TPU v7x, 32 devices: a whole 2x2x4 slice. The times are simulated.
32 devices in a mesh: case: 2 (over y), mode: 4 (over z), harm: 2 (over x), rad: 2 (over core).
Axes of the slice: x: 2, y: 2, z: 4, core: 2. Of those that a mesh axis runs over, the one named last changes fastest.
Arguments:
- direct_field: bfloat16 [16, 16, 2, 5, 16, 256], P(('case', 'harm'), 'mode', None, None, None, 'rad'), parts along dimension 0, may hold values from -6 to 6
- adjoint_field: bfloat16 [16, 16, 2, 5, 16, 256], P(('case', 'harm'), 'mode', None, None, None, 'rad'), parts along dimension 0, may hold values from -6 to 6
- triad_slots: int32 [16, 4, 2], P('mode'), may hold values from 0 to 3
Outputs:
- sensitivity: float32 [32, 2, 5, 16, 256], P(('case', 'harm'), None, None, 'mode', 'rad'), parts along dimension 0
There are 2 independent parts, one for each index of `case`. A program takes and returns all parts, laid end to end along the dimension named above; an argument that names none is the same for every part. Nothing has to cross between parts.
Inputs may be any that keep to these rules, and one draw needn't show every extreme that they name: triad_slots[m, s, 0] is the slot, within the block of 4 modes holding m, of the adjoint factor; triad_slots[m, s, 1] is the slot of the direct factor within the block s blocks below m's block, counted cyclically over 4 blocks.
All inputs are finite; a program needn't handle non-finite values.
Results may differ from a plain program's by a relative error of at most 0.0003.
Values may be sent and summed in bfloat16 or wider, within the bound.
A program may use at most 64 MiB of HBM per device.

v0:
```python
import math

import jax
import jax.numpy as jnp
from jax import lax
from jax.sharding import PartitionSpec as P

HARMS = 8


def padded_2(block, sides, width):
    for axis, dim in sides:
        count = lax.axis_size(axis)
        forward = [(i, i + 1) for i in range(count - 1)]
        backward = [(target, source) for source, target in forward]
        low = lax.ppermute(
            lax.slice_in_dim(block, block.shape[dim] - width, None, axis=dim), axis, forward
        )
        high = lax.ppermute(lax.slice_in_dim(block, 0, width, axis=dim), axis, backward)
        block = jnp.concatenate([low, block, high], axis=dim)
    return block


def passed_along(value, axis, steps):
    count = lax.axis_size(axis)
    pairs = [(source, (source + steps) % count) for source in range(count)]
    return lax.ppermute(value, axis, pairs)


def stencil(padded, axis, length):

    def shifted(offset):
        return lax.slice_in_dim(padded, offset, offset + length, axis=axis)

    return (shifted(0) - 8.0 * shifted(1) + 8.0 * shifted(3) - shifted(4)) / 12.0


def derivative(source, axis):
    length = source.shape[axis]
    widths = [(0, 0)] * source.ndim
    widths[axis] = (2, 2)
    return stencil(jnp.pad(source, widths), axis, length)


def conj_product(left_side, right_side):
    left_real = left_side[..., 0, :, :, :]
    left_imag = left_side[..., 1, :, :, :]
    right_real = right_side[..., 0, :, :, :]
    right_imag = right_side[..., 1, :, :, :]
    return jnp.stack(
        [
            left_real * right_real + left_imag * right_imag,
            left_real * right_imag - left_imag * right_real,
        ],
        axis=-4,
    )


def triad_term(adjoint, adjoint_axial, adjoint_radial, direct, direct_axial, direct_radial):
    total_sum = conj_product(direct[..., 1:2, :, :], adjoint_axial)
    total_sum = total_sum + conj_product(direct[..., 2:3, :, :], adjoint_radial)
    total_sum = total_sum + conj_product(direct_axial, adjoint[..., 1:2, :, :])
    return total_sum + conj_product(direct_radial, adjoint[..., 2:3, :, :])


def choose(source, picked_rows):
    slot_count = source.shape[1]
    wanted = picked_rows.reshape((1, slot_count, 1, 1, 1, 1))
    picked = jnp.zeros(source.shape, jnp.float32)
    for slot_index in range(slot_count):
        candidate = lax.slice_in_dim(source, slot_index, slot_index + 1, axis=1)
        picked = picked + jnp.where(wanted == slot_index, candidate, 0.0)
    return picked


def body(direct_field, adjoint_field, triad_slots):
    stop_count = lax.axis_size("mode")
    radial_cells = adjoint_field.shape[5]
    adjoint = adjoint_field.astype(jnp.float32)
    adjoint_axial = derivative(adjoint, 4)
    adjoint_wide = padded_2(adjoint_field, (("rad", 5),), 2)
    adjoint_radial = stencil(adjoint_wide.astype(jnp.float32), 5, radial_cells)
    adjoint_slots = triad_slots[:, :, 0]
    direct_slots = triad_slots[:, :, 1]

    def add_stop(running, visiting, stop_index):
        direct_core = lax.slice_in_dim(visiting, 2, 2 + radial_cells, axis=5)
        direct = direct_core.astype(jnp.float32)
        direct_axial = derivative(direct, 4)
        direct_radial = stencil(visiting.astype(jnp.float32), 5, radial_cells)
        adjoint_rows = lax.dynamic_index_in_dim(adjoint_slots, stop_index, axis=1, keepdims=False)
        direct_rows = lax.dynamic_index_in_dim(direct_slots, stop_index, axis=1, keepdims=False)
        term = triad_term(
            choose(adjoint, adjoint_rows),
            choose(adjoint_axial, adjoint_rows),
            choose(adjoint_radial, adjoint_rows),
            choose(direct, direct_rows),
            choose(direct_axial, direct_rows),
            choose(direct_radial, direct_rows),
        )
        return running + jnp.sum(term, axis=0)

    start_block = padded_2(direct_field, (("rad", 5),), 2)
    running = jnp.zeros(adjoint.shape[1:], jnp.float32)

    def one_side(step_index, carry):
        running_sum, visiting = carry
        arriving = passed_along(visiting, "mode", 1)
        running_sum = add_stop(running_sum, visiting, step_index)
        return (running_sum, arriving)

    running, visiting = lax.fori_loop(0, stop_count - 1, one_side, (running, start_block))
    running = add_stop(running, visiting, stop_count - 1)
    slabs = lax.all_to_all(running, "mode", split_axis=3, concat_axis=0, tiled=True)
    summed = lax.psum_scatter(slabs, "harm", scatter_dimension=0, tiled=True)
    return summed * (1.0 / math.sqrt(8.0 * stop_count * HARMS))


def solution(mesh):
    return jax.shard_map(
        body,
        mesh=mesh,
        in_specs=(
            P(("case", "harm"), "mode", None, None, None, "rad"),
            P(("case", "harm"), "mode", None, None, None, "rad"),
            P("mode", None, None),
        ),
        out_specs=P(("case", "harm"), None, None, "mode", "rad"),
        check_vma=False,
    )
```

profile of v0, /device:TPU:0, one launch (start us, length us, event | category | flops | bytes accessed | tf_op | source)
XLA Modules:
  0.0 197.8 jit_solution(2446714134375759526)
XLA Ops:
  11.5 3.7 %collective-permute-start.1 = (bf16[4,4,2,5,16,2]{4,1,5,3,2,0:T(4,128)(2,1)S(1)}, bf16[4,4,2,5,16,2]{4,1,5,3,2,0:T(4,128)(2,1)}, u32[]{:S(2)}, u32[]{:S(2)}) collective-permute-start(bf16[4,4,2,5,16,2]{4,1,5,3,2,0:T(4,128)(2,1)S(1)} %copy.49), channel_id=1, source_target_pairs={{0,1},{2,3},{4,5},{6,7},{8,9},{10,11},{12,13},{14,15},{16,17},{18,... | collective-permute-start | bytes 30728 | tf_op jit(solution)/shard_map/ppermute | solution.py:16
  18.8 4.0 %collective-permute-start.3 = (bf16[4,4,2,5,16,2]{4,1,5,3,2,0:T(4,128)(2,1)S(1)}, bf16[4,4,2,5,16,2]{4,1,5,3,2,0:T(4,128)(2,1)S(1)}, u32[]{:S(2)}, u32[]{:S(2)}) collective-permute-start(bf16[4,4,2,5,16,2]{4,1,5,3,2,0:T(4,128)(2,1)S(1)} %copy.51), channel_id=1, source_target_pairs={{0,1},{2,3},{4,5},{6,7},{8,9},{10,11},{12,13},{14,15},{16,17},{18,... | collective-permute-start | bytes 30728 | tf_op jit(solution)/shard_map/ppermute | solution.py:16
  26.7 1.9 copy.44
  29.3 2.7 %fusion.15 = (f32[4,4,2,5,16,128]{5,4,3,2,0,1:T(8,128)}, f32[4,4,2,5,16,128]{5,4,3,2,0,1:T(8,128)}) fusion(f32[4,4,2,5,16,128]{5,4,3,2,0,1:T(8,128)S(1)} %get-tuple-element.587, f32[4,4,2,5,16,132]{5,4,3,2,0,1:T(8,128)S(1)} %maximum_convert_fusion), kind=kLoop, calls=%fused_computation.89 | loop fusion | flops 3932160 | bytes 9175040 | tf_op jit(solution)/shard_map/div | solution.py:35
  32.0 2.0 %copy.36 = bf16[4,4,2,5,16,2]{5,4,3,2,0,1:T(8,128)(2,1)S(1)} copy(bf16[4,4,2,5,16,2]{4,1,5,3,2,0:T(4,128)(2,1)} %collective-permute-done.1) | data formatting | bytes 20480 | tf_op jit(solution)/shard_map/ppermute | solution.py:16
  35.0 1.8 pad_maximum_fusion
  36.8 105.0 %while.18 = (s32[]{:T(128)}, f32[4,2,5,16,128]{4,3,2,1,0:T(8,128)}, bf16[4,4,2,5,16,132]{5,4,3,2,0,1:T(8,128)(2,1)}, s32[4,4]{0,1:T(4,128)S(1)}, s32[4,4]{0,1:T(...) while((s32[]{:T(128)}, f32[4,2,5,16,128]{4,3,2,1,0:T(8,128)}, ...), condition=%wide.region_2.3_spmd.clone, body=%wide.region_0.2_spmd.clone.sunk | while | flops 24995872 | bytes 105566816 | solution.py:112
  36.8 3.0 %copy.62 = bf16[4,4,2,5,16,132]{5,4,3,2,0,1:T(8,128)(2,1)} copy(bf16[4,4,2,5,16,132]{5,4,3,2,0,1:T(8,128)(2,1)} %get-tuple-element.592) | data formatting | bytes 1351680 | tf_op jit(solution)/shard_map/while
  39.9 3.0 %collective-permute-start = (bf16[4,4,2,5,16,132]{5,4,3,2,0,1:T(8,128)(2,1)}, bf16[4,4,2,5,16,132]{5,4,3,2,0,1:T(8,128)(2,1)}, u32[]{:S(2)}, u32[]{:S(2)}) collective-permute-start(bf16[4,4,2,5,16,132]{5,4,3,2,0,1:T(8,128)(2,1)} %copy.62), channel_id=1, source_target_pairs={{0,4},{4,8},{8,12},{12,0},{1,5},{5,9},{9,13},{13,1},{2,6},{6,10},{... | collective-permute-start | bytes 2027528 | tf_op jit(solution)/shard_map/while/body/eval_jaxpr/ppermute | solution.py:27
  44.5 1.7 fusion.42
  47.2 1.7 convert_element_type.55
  61.0 12.6 %collective-permute-done = bf16[4,4,2,5,16,132]{5,4,3,2,0,1:T(8,128)(2,1)} collective-permute-done((bf16[4,4,2,5,16,132]{5,4,3,2,0,1:T(8,128)(2,1)}, bf16[4,4,2,5,16,132]{5,4,3,2,0,1:T(8,128)(2,1)}, u32[]{:S(2)}, u32[]{:S(2)}) %collective-permute-start) | collective-permute-done | bytes 675872 | tf_op jit(solution)/shard_map/while/body/eval_jaxpr/ppermute | solution.py:27
  73.6 3.0 %copy.62 = bf16[4,4,2,5,16,132]{5,4,3,2,0,1:T(8,128)(2,1)} copy(bf16[4,4,2,5,16,132]{5,4,3,2,0,1:T(8,128)(2,1)} %get-tuple-element.592) | data formatting | bytes 1351680 | tf_op jit(solution)/shard_map/while
  78.2 1.7 fusion.42
  80.9 1.7 convert_element_type.55
  93.9 1.8 select_add_fusion.18
  95.6 12.5 %collective-permute-done = bf16[4,4,2,5,16,132]{5,4,3,2,0,1:T(8,128)(2,1)} collective-permute-done((bf16[4,4,2,5,16,132]{5,4,3,2,0,1:T(8,128)(2,1)}, bf16[4,4,2,5,16,132]{5,4,3,2,0,1:T(8,128)(2,1)}, u32[]{:S(2)}, u32[]{:S(2)}) %collective-permute-start) | collective-permute-done | bytes 675872 | tf_op jit(solution)/shard_map/while/body/eval_jaxpr/ppermute | solution.py:27
  108.1 3.0 %copy.62 = bf16[4,4,2,5,16,132]{5,4,3,2,0,1:T(8,128)(2,1)} copy(bf16[4,4,2,5,16,132]{5,4,3,2,0,1:T(8,128)(2,1)} %get-tuple-element.592) | data formatting | bytes 1351680 | tf_op jit(solution)/shard_map/while
  112.8 1.7 fusion.42
  115.4 1.7 convert_element_type.55
  128.4 1.8 select_add_fusion.18
  130.2 11.6 %collective-permute-done = bf16[4,4,2,5,16,132]{5,4,3,2,0,1:T(8,128)(2,1)} collective-permute-done((bf16[4,4,2,5,16,132]{5,4,3,2,0,1:T(8,128)(2,1)}, bf16[4,4,2,5,16,132]{5,4,3,2,0,1:T(8,128)(2,1)}, u32[]{:S(2)}, u32[]{:S(2)}) %collective-permute-start) | collective-permute-done | bytes 675872 | tf_op jit(solution)/shard_map/while/body/eval_jaxpr/ppermute | solution.py:27
  155.1 10.4 %all_to_all.18 = f32[4,2,5,16,128]{4,0,2,1,3:T(4,128)S(1)} all-to-all(f32[4,2,5,16,128]{4,0,2,1,3:T(4,128)S(1)} %copy.47), channel_id=1, replica_groups=mesh['case'=2,'mode'=4,'harm'=2,'rad'=2] {'mode'}, dimensions={3} | all-to-all | bytes 655360 | tf_op jit(solution)/shard_map/all_to_all | solution.py:114
  167.5 21.8 %all-reduce.6.cloned.1.call-done = f32[16,2,5,4,128]{4,3,2,1,0:T(4,128)} async-done(((f32[16,2,5,4,128]{4,3,2,1,0:T(4,128)}), f32[16,2,5,4,128]{4,3,2,1,0:T(4,128)}) %all-reduce.6.cloned.1.call-update) | async-done | bytes 327696
  (196 shorter events, 72.4 us)
Async XLA Ops:
  6.5 182.8 %all-reduce.6.cloned.1.call-start = ((), (), s32[]{:S(2)}) async-start(), calls=%async_computation.1 | async-start | bytes 655360
  8.1 7.1 %copy-start.12 = (bf16[4,4,2,5,16,128]{5,4,3,2,1,0:T(8,128)(2,1)S(1)}, bf16[4,4,2,5,16,128]{5,4,3,2,1,0:T(8,128)(2,1)}, u32[]{:S(2)}) copy-start(bf16[4,4,2,5,16,128]{5,4,3,2,1,0:T(8,128)(2,1)} %param.6) | copy-start | bytes 1966084
  9.1 24.8 %collective-permute-start.2 = (bf16[4,4,2,5,16,2]{4,1,5,3,2,0:T(4,128)(2,1)S(1)}, bf16[4,4,2,5,16,2]{4,1,5,3,2,0:T(4,128)(2,1)S(1)}, u32[]{:S(2)}, u32[]{:S(2)}) collective-permute-start(bf16[4,4,2,5,16,2]{4,1,5,3,2,0:T(4,128)(2,1)S(1)} %copy.50), channel_id=1, source_target_pairs={{1,0},{3,2},{5,4},{7,6},{9,8},{11,10},{13,12},{15,14},{17,16},{19,... | collective-permute-start | bytes 30728 | tf_op jit(solution)/shard_map/ppermute | solution.py:19
  11.5 20.5 %collective-permute-start.1 = (bf16[4,4,2,5,16,2]{4,1,5,3,2,0:T(4,128)(2,1)S(1)}, bf16[4,4,2,5,16,2]{4,1,5,3,2,0:T(4,128)(2,1)}, u32[]{:S(2)}, u32[]{:S(2)}) collective-permute-start(bf16[4,4,2,5,16,2]{4,1,5,3,2,0:T(4,128)(2,1)S(1)} %copy.49), channel_id=1, source_target_pairs={{0,1},{2,3},{4,5},{6,7},{8,9},{10,11},{12,13},{14,15},{16,17},{18,... | collective-permute-start | bytes 30728 | tf_op jit(solution)/shard_map/ppermute | solution.py:16
  16.5 10.2 %collective-permute-start.4 = (bf16[4,4,2,5,16,2]{4,1,5,3,2,0:T(4,128)(2,1)S(1)}, bf16[4,4,2,5,16,2]{4,1,5,3,2,0:T(4,128)(2,1)}, u32[]{:S(2)}, u32[]{:S(2)}) collective-permute-start(bf16[4,4,2,5,16,2]{4,1,5,3,2,0:T(4,128)(2,1)S(1)} %copy.52), channel_id=1, source_target_pairs={{1,0},{3,2},{5,4},{7,6},{9,8},{11,10},{13,12},{15,14},{17,16},{19,... | collective-permute-start | bytes 30728 | tf_op jit(solution)/shard_map/ppermute | solution.py:19
  18.8 4.2 %copy-start.18 = (s32[4,4,2]{1,2,0:T(2,128)S(1)}, s32[4,4,2]{1,2,0:T(2,128)}, u32[]{:S(2)}) copy-start(s32[4,4,2]{1,2,0:T(2,128)} %param.7) | copy-start | bytes 388
  18.8 6.8 %collective-permute-start.3 = (bf16[4,4,2,5,16,2]{4,1,5,3,2,0:T(4,128)(2,1)S(1)}, bf16[4,4,2,5,16,2]{4,1,5,3,2,0:T(4,128)(2,1)S(1)}, u32[]{:S(2)}, u32[]{:S(2)}) collective-permute-start(bf16[4,4,2,5,16,2]{4,1,5,3,2,0:T(4,128)(2,1)S(1)} %copy.51), channel_id=1, source_target_pairs={{0,1},{2,3},{4,5},{6,7},{8,9},{10,11},{12,13},{14,15},{16,17},{18,... | collective-permute-start | bytes 30728 | tf_op jit(solution)/shard_map/ppermute | solution.py:16
  32.0 3.0 %copy-start.13 = (bf16[4,4,2,5,16,128]{5,4,3,2,1,0:T(8,128)(2,1)S(1)}, bf16[4,4,2,5,16,128]{5,4,3,2,1,0:T(8,128)(2,1)}, u32[]{:S(2)}) copy-start(bf16[4,4,2,5,16,128]{5,4,3,2,1,0:T(8,128)(2,1)} %param.5) | copy-start | bytes 1966084
  36.8 3.0 %copy-start.1 = (f32[4,4,2,5,16,128]{5,4,3,2,0,1:T(8,128)}, f32[4,4,2,5,16,128]{5,4,3,2,0,1:T(8,128)S(1)}, u32[]{:S(2)}) copy-start(f32[4,4,2,5,16,128]{5,4,3,2,0,1:T(8,128)S(1)} %get-tuple-element.607) | copy-start | bytes 3932164 | tf_op jit(solution)/shard_map/while
  39.9 33.7 %collective-permute-start = (bf16[4,4,2,5,16,132]{5,4,3,2,0,1:T(8,128)(2,1)}, bf16[4,4,2,5,16,132]{5,4,3,2,0,1:T(8,128)(2,1)}, u32[]{:S(2)}, u32[]{:S(2)}) collective-permute-start(bf16[4,4,2,5,16,132]{5,4,3,2,0,1:T(8,128)(2,1)} %copy.62), channel_id=1, source_target_pairs={{0,4},{4,8},{8,12},{12,0},{1,5},{5,9},{9,13},{13,1},{2,6},{6,10},{... | collective-permute-start | bytes 2027528 | tf_op jit(solution)/shard_map/while/body/eval_jaxpr/ppermute | solution.py:27
  52.6 1.7 copy-start.7
  58.2 1.5 copy-start.6
  59.6 13.9 %copy-start.3 = (f32[4,4,2,5,16,128]{5,4,3,2,0,1:T(8,128)S(1)}, f32[4,4,2,5,16,128]{5,4,3,2,0,1:T(8,128)}, u32[]{:S(2)}) copy-start(f32[4,4,2,5,16,128]{5,4,3,2,0,1:T(8,128)} %copy-done.1) | copy-start | bytes 3932164 | tf_op jit(solution)/shard_map/while
  73.6 3.0 %copy-start.1 = (f32[4,4,2,5,16,128]{5,4,3,2,0,1:T(8,128)}, f32[4,4,2,5,16,128]{5,4,3,2,0,1:T(8,128)S(1)}, u32[]{:S(2)}) copy-start(f32[4,4,2,5,16,128]{5,4,3,2,0,1:T(8,128)S(1)} %get-tuple-element.607) | copy-start | bytes 3932164 | tf_op jit(solution)/shard_map/while
  76.6 31.6 %collective-permute-start = (bf16[4,4,2,5,16,132]{5,4,3,2,0,1:T(8,128)(2,1)}, bf16[4,4,2,5,16,132]{5,4,3,2,0,1:T(8,128)(2,1)}, u32[]{:S(2)}, u32[]{:S(2)}) collective-permute-start(bf16[4,4,2,5,16,132]{5,4,3,2,0,1:T(8,128)(2,1)} %copy.62), channel_id=1, source_target_pairs={{0,4},{4,8},{8,12},{12,0},{1,5},{5,9},{9,13},{13,1},{2,6},{6,10},{... | collective-permute-start | bytes 2027528 | tf_op jit(solution)/shard_map/while/body/eval_jaxpr/ppermute | solution.py:27
  86.3 1.7 copy-start.7
  91.9 1.5 copy-start.6
  93.3 14.8 %copy-start.3 = (f32[4,4,2,5,16,128]{5,4,3,2,0,1:T(8,128)S(1)}, f32[4,4,2,5,16,128]{5,4,3,2,0,1:T(8,128)}, u32[]{:S(2)}) copy-start(f32[4,4,2,5,16,128]{5,4,3,2,0,1:T(8,128)} %copy-done.1) | copy-start | bytes 3932164 | tf_op jit(solution)/shard_map/while
  108.1 3.0 %copy-start.1 = (f32[4,4,2,5,16,128]{5,4,3,2,0,1:T(8,128)}, f32[4,4,2,5,16,128]{5,4,3,2,0,1:T(8,128)S(1)}, u32[]{:S(2)}) copy-start(f32[4,4,2,5,16,128]{5,4,3,2,0,1:T(8,128)S(1)} %get-tuple-element.607) | copy-start | bytes 3932164 | tf_op jit(solution)/shard_map/while
  111.2 30.6 %collective-permute-start = (bf16[4,4,2,5,16,132]{5,4,3,2,0,1:T(8,128)(2,1)}, bf16[4,4,2,5,16,132]{5,4,3,2,0,1:T(8,128)(2,1)}, u32[]{:S(2)}, u32[]{:S(2)}) collective-permute-start(bf16[4,4,2,5,16,132]{5,4,3,2,0,1:T(8,128)(2,1)} %copy.62), channel_id=1, source_target_pairs={{0,4},{4,8},{8,12},{12,0},{1,5},{5,9},{9,13},{13,1},{2,6},{6,10},{... | collective-permute-start | bytes 2027528 | tf_op jit(solution)/shard_map/while/body/eval_jaxpr/ppermute | solution.py:27
  120.9 1.7 copy-start.7
  126.4 1.5 copy-start.6
  127.9 13.9 %copy-start.3 = (f32[4,4,2,5,16,128]{5,4,3,2,0,1:T(8,128)S(1)}, f32[4,4,2,5,16,128]{5,4,3,2,0,1:T(8,128)}, u32[]{:S(2)}) copy-start(f32[4,4,2,5,16,128]{5,4,3,2,0,1:T(8,128)} %copy-done.1) | copy-start | bytes 3932164 | tf_op jit(solution)/shard_map/while
  154.8 11.5 %copy-start.25 = (u32[32]{0:T(128)S(1)}, u32[32]{0:T(128)}, u32[]{:S(2)}) copy-start(u32[32]{0:T(128)} %constant.132) | copy-start | bytes 388
  (30 other events, 33.7 us)
Sparse Core Ops, SparseCore 0:
  166.4 22.8 all-reduce.5
where the time goes:
time: 199 us; the launch traced here: 198 us
  waiting for transfers between devices  58.5 us (29%)
  other arithmetic  56 us (28%)
  local copies, waits for them, and re-layouts  44.9 us (23%)
  between operations  14.4 us (7%)
  starting transfers between devices  13.3 us (7%)
  blocking collectives  10.4 us (5%)
    ppermute x3, waiting for transfers between devices, passed_along(): return lax.ppermute(value, axis, pairs)  36.7 us
    unnamed x2, waiting for transfers between devices  21.8 us
    while x63, local copies, waits for them, and re-layouts  17.8 us
    div x9, other arithmetic, stencil(): (shifted(0) - 8.0 * shifted(1) + 8.0 * shifted(3) - shifted(4)) / 12.0  12.6 us
    all_to_all x1, blocking collectives, body(): lax.all_to_all(running, 'mode', split_axis=3, concat_axis=0, tiled=True)  10.4 us
    broadcast_in_dim x18, local copies, waits for them, and re-layouts, choose(): picked = picked + jnp.where(wanted == slot_index, candidate, 0.0)  9.97 us
    add x8, other arithmetic, choose(): picked = picked + jnp.where(wanted == slot_index, candidate, 0.0)  8.58 us
    add x16, other arithmetic, conj_product(): left_real * right_real + left_imag * right_imag  8.58 us
  transfers between devices with their start and end apart: 8, of which 4 were waited for; matrix products, arithmetic and copies ran while one was open for 31% of the time, Pallas kernels for 0%

commit v1 on v0

v1 whole, which is shorter than its diff:
```python
import functools
import math

import jax
import jax.numpy as jnp
from jax import lax
from jax.experimental import pallas as pl
from jax.experimental.pallas import tpu as pltpu
from jax.sharding import PartitionSpec as P

HARMS = 8
SLOTS = 4
FIELDS = 5
PLANES = 2 * FIELDS
MESH = pl.DeviceIdType.MESH


def coefficient(offset):
    value = jnp.where(offset == 1, 8.0, 0.0)
    value = jnp.where(offset == -1, -8.0, value)
    value = jnp.where(offset == 2, -1.0, value)
    value = jnp.where(offset == -2, 1.0, value)
    return value


def kernel(
    n, hs, kh, nx,
    slots, d_ref, a_ref, out_ref,
    gbuf, pbuf, apbuf,
    d_st, dx_st, dr_st, a_st, ax_st, ar_st,
    run, sbuf, rbuf, radial, axial,
    right_send, right_recv, left_send, left_recv,
    core_send, core_recv, adj_sem, slab_send, slab_recv,
):
    me = lax.axis_index("mode")
    my_harm = lax.axis_index("harm")
    core = lax.axis_index("rad")
    per_owner = n // hs
    cells = nx // n
    rows = d_ref.shape[0]
    chunk = axial.shape[0]

    barrier = pltpu.get_barrier_semaphore()

    def greet(index, carry):
        q = index // hs
        h = index % hs

        @pl.when(jnp.logical_or(q != me, h != my_harm))
        def _():
            pl.semaphore_signal(barrier, inc=1, device_id={"mode": q, "harm": h}, device_id_type=MESH)

        return carry

    lax.fori_loop(0, n * hs, greet, 0)
    pl.semaphore_signal(barrier, inc=1, device_id={"rad": 1 - core}, device_id_type=MESH)
    pl.semaphore_wait(barrier, n * hs)

    def to_right(src, block, hop):
        return pltpu.make_async_remote_copy(
            src_ref=src, dst_ref=gbuf.at[block],
            send_sem=right_send.at[hop], recv_sem=right_recv.at[hop],
            device_id={"mode": me + 1}, device_id_type=MESH)

    def to_left(src, block, hop):
        return pltpu.make_async_remote_copy(
            src_ref=src, dst_ref=gbuf.at[block],
            send_sem=left_send.at[hop], recv_sem=left_recv.at[hop],
            device_id={"mode": me - 1}, device_id_type=MESH)

    def to_core(src, block):
        return pltpu.make_async_remote_copy(
            src_ref=src, dst_ref=pbuf.at[block],
            send_sem=core_send.at[block], recv_sem=core_recv.at[block],
            device_id={"rad": 1 - core}, device_id_type=MESH)

    adj_copy = pltpu.make_async_remote_copy(
        src_ref=a_ref, dst_ref=apbuf, send_sem=adj_sem.at[0], recv_sem=adj_sem.at[1],
        device_id={"rad": 1 - core}, device_id_type=MESH)

    @pl.when(me < n - 1)
    def _():
        to_right(d_ref, me, 0).start()

    @pl.when(me > 0)
    def _():
        to_left(d_ref, me, 0).start()

    adj_copy.start()
    to_core(d_ref, me).start()

    row = lax.broadcasted_iota(jnp.int32, (128, 128), 0)
    col = lax.broadcasted_iota(jnp.int32, (128, 128), 1)
    shift = (1 - 2 * core) * 128
    radial[0:128, :] = coefficient(row - col).astype(jnp.bfloat16)
    radial[128:256, :] = coefficient(row - col + shift).astype(jnp.bfloat16)
    row = lax.broadcasted_iota(jnp.int32, (chunk, chunk), 0)
    col = lax.broadcasted_iota(jnp.int32, (chunk, chunk), 1)
    same = (row // nx) == (col // nx)
    axial[...] = jnp.where(same, coefficient(col - row), 0.0).astype(jnp.bfloat16)
    run[...] = jnp.zeros_like(run)

    def prepare(own, partner, plain, along_x, along_r):
        def step(i, carry):
            at = pl.ds(pl.multiple_of(i * chunk, chunk), chunk)
            planes = pl.ds(i * (chunk // nx), chunk // nx)
            mine = own[at, :]
            both = jnp.concatenate([mine, partner[at, :]], axis=1)
            shape = (chunk // nx, nx, 128)
            plain[planes] = mine.astype(jnp.float32).reshape(shape)
            along_r[planes] = jnp.dot(
                both, radial[...], preferred_element_type=jnp.float32).reshape(shape)
            along_x[planes] = jnp.dot(
                axial[...], mine, preferred_element_type=jnp.float32).reshape(shape)
            return carry

        lax.fori_loop(0, rows // chunk, step, 0)

    def products(stop):
        def one_mode(m, carry):
            adj_slot = slots[m, stop, 0]
            dir_slot = slots[m, stop, 1]
            for half in range(nx // 8):
                part = pl.ds(half * 8, 8)
                real = [run[m * PLANES + f, part, :] for f in range(FIELDS)]
                imag = [run[m * PLANES + FIELDS + f, part, :] for f in range(FIELDS)]
                for k in range(kh):
                    da = (k * SLOTS + adj_slot) * PLANES
                    dd = (k * SLOTS + dir_slot) * PLANES
                    d1r = d_st[dd + 1, part, :]
                    d2r = d_st[dd + 2, part, :]
                    d1i = d_st[dd + FIELDS + 1, part, :]
                    d2i = d_st[dd + FIELDS + 2, part, :]
                    a1r = a_st[da + 1, part, :]
                    a2r = a_st[da + 2, part, :]
                    a1i = a_st[da + FIELDS + 1, part, :]
                    a2i = a_st[da + FIELDS + 2, part, :]
                    for f in range(FIELDS):
                        axr = ax_st[da + f, part, :]
                        axi = ax_st[da + FIELDS + f, part, :]
                        arr = ar_st[da + f, part, :]
                        ari = ar_st[da + FIELDS + f, part, :]
                        dxr = dx_st[dd + f, part, :]
                        dxi = dx_st[dd + FIELDS + f, part, :]
                        drr = dr_st[dd + f, part, :]
                        dri = dr_st[dd + FIELDS + f, part, :]
                        real[f] = real[f] + (
                            ((d1r * axr + d1i * axi) + (d2r * arr + d2i * ari))
                            + ((dxr * a1r + dxi * a1i) + (drr * a2r + dri * a2i)))
                        imag[f] = imag[f] + (
                            ((d1r * axi - d1i * axr) + (d2r * ari - d2i * arr))
                            + ((dxr * a1i - dxi * a1r) + (drr * a2i - dri * a2r)))
                for f in range(FIELDS):
                    run[m * PLANES + f, part, :] = real[f]
                    run[m * PLANES + FIELDS + f, part, :] = imag[f]
            return carry

        lax.fori_loop(0, SLOTS, one_mode, 0)

    def visit(block, stop):
        to_core(gbuf.at[block], block).wait_recv()
        prepare(gbuf.at[block], pbuf.at[block], d_st, dx_st, dr_st)
        products(stop)

    def hop_step(hop, carry):
        from_left = me - hop
        from_right = me + hop

        @pl.when(from_left >= 0)
        def _():
            to_right(gbuf.at[from_left], from_left, hop - 1).wait_recv()
            to_core(gbuf.at[from_left], from_left).start()

            @pl.when(me < n - 1)
            def _():
                to_right(gbuf.at[from_left], from_left, hop).start()

        @pl.when(from_right < n)
        def _():
            to_left(gbuf.at[from_right], from_right, hop - 1).wait_recv()
            to_core(gbuf.at[from_right], from_right).start()

            @pl.when(me > 0)
            def _():
                to_left(gbuf.at[from_right], from_right, hop).start()

        return carry

    def visit_hop(hop):
        @pl.when(me - hop >= 0)
        def _():
            visit(me - hop, hop)

        @pl.when(me + hop < n)
        def _():
            visit(me + hop, n - hop)

    adj_copy.wait_recv()
    prepare(a_ref, apbuf, a_st, ax_st, ar_st)
    to_core(d_ref, me).wait_recv()
    prepare(d_ref, pbuf.at[me], d_st, dx_st, dr_st)
    products(0)

    def steps(hop, carry):
        @pl.when(hop < n)
        def _():
            hop_step(hop, 0)

        @pl.when(hop > 1)
        def _():
            visit_hop(hop - 1)

        return carry

    lax.fori_loop(1, n + 1, steps, 0)

    scale = 1.0 / (12.0 * math.sqrt(8.0 * n * HARMS))
    for q in range(n):
        sbuf[q] = run[:, q * cells:(q + 1) * cells, :] * scale

    owner = me // per_owner
    place = me % per_owner

    def slab(q, h, i):
        return pltpu.make_async_remote_copy(
            src_ref=sbuf.at[q], dst_ref=rbuf.at[h * per_owner + i],
            send_sem=slab_send.at[q], recv_sem=slab_recv.at[h * per_owner + i],
            device_id={"mode": q, "harm": owner}, device_id_type=MESH)

    def each_target(act):
        def step(q, carry):
            @pl.when(jnp.logical_or(q != me, owner != my_harm))
            def _():
                act(slab(q, my_harm, place))

            return carry

        lax.fori_loop(0, n, step, 0)

    each_target(lambda copy: copy.start())

    @pl.when(owner == my_harm)
    def _():
        rbuf[my_harm * per_owner + place] = sbuf[me]

    def arrive(index, carry):
        h = index // per_owner
        i = index % per_owner
        mine = jnp.logical_and(h == my_harm, my_harm * per_owner + i == me)

        @pl.when(jnp.logical_not(mine))
        def _():
            slab(0, h, i).wait_recv()

        return carry

    lax.fori_loop(0, hs * per_owner, arrive, 0)
    for i in range(per_owner):
        total = rbuf[i]
        for h in range(1, hs):
            total = total + rbuf[h * per_owner + i]
        out_ref[i] = total

    each_target(lambda copy: copy.wait_send())
    adj_copy.wait_send()

    def drain(block, carry):
        to_core(d_ref, block).wait_send()
        return carry

    lax.fori_loop(0, n, drain, 0)

    def drain_hops(hop, carry):
        @pl.when(jnp.logical_and(me - hop >= 0, me < n - 1))
        def _():
            to_right(d_ref, me, hop).wait_send()

        @pl.when(jnp.logical_and(me + hop < n, me > 0))
        def _():
            to_left(d_ref, me, hop).wait_send()

        return carry

    lax.fori_loop(0, n, drain_hops, 0)


def body(hs, direct_field, adjoint_field, triad_slots):
    n = triad_slots.shape[1]
    kh = direct_field.shape[0]
    nx = direct_field.shape[4]
    planes = kh * SLOTS * PLANES
    rows = planes * nx
    chunk = 256 if rows % 256 == 0 else 128
    cells = nx // n
    per_owner = n // hs
    f32, bf16 = jnp.float32, jnp.bfloat16
    dma = pltpu.SemaphoreType.DMA
    out = pl.pallas_call(
        functools.partial(kernel, n, hs, kh, nx),
        out_shape=jax.ShapeDtypeStruct((per_owner, SLOTS * PLANES, cells, 128), f32),
        in_specs=[pl.BlockSpec(memory_space=pltpu.SMEM)] + [pl.BlockSpec(memory_space=pltpu.VMEM)] * 2,
        out_specs=pl.BlockSpec(memory_space=pltpu.VMEM),
        scratch_shapes=[
            pltpu.VMEM((n, rows, 128), bf16),
            pltpu.VMEM((n, rows, 128), bf16),
            pltpu.VMEM((rows, 128), bf16),
        ] + [pltpu.VMEM((planes, nx, 128), f32)] * 6 + [
            pltpu.VMEM((SLOTS * PLANES, nx, 128), f32),
            pltpu.VMEM((n, SLOTS * PLANES, cells, 128), f32),
            pltpu.VMEM((hs * per_owner, SLOTS * PLANES, cells, 128), f32),
            pltpu.VMEM((256, 128), bf16),
            pltpu.VMEM((chunk, chunk), bf16),
            dma((n,)), dma((n,)), dma((n,)), dma((n,)),
            dma((n,)), dma((n,)), dma((2,)), dma((n,)), dma((hs * per_owner,)),
        ],
        compiler_params=pltpu.CompilerParams(
            collective_id=0, has_side_effects=True, vmem_limit_bytes=50 << 20),
    )(
        triad_slots,
        direct_field.reshape(rows, 128),
        adjoint_field.reshape(rows, 128),
    )
    return out.reshape(per_owner * SLOTS, 2, FIELDS, cells, 128)


def solution(mesh):
    return jax.shard_map(
        functools.partial(body, mesh.shape["harm"]),
        mesh=mesh,
        in_specs=(
            P(("case", "harm"), "mode", None, None, None, "rad"),
            P(("case", "harm"), "mode", None, None, None, "rad"),
            P("mode", None, None),
        ),
        out_specs=P(("case", "harm"), None, None, "mode", "rad"),
        check_vma=False,
    )
```

time: 199 us -> 68.7 us (0.35)
  Pallas kernels: 0 us -> 64.8 us
  waiting for transfers between devices: 58.5 us -> 0 us
  other arithmetic: 56 us -> 0 us
  local copies, waits for them, and re-layouts: 44.9 us -> 3.63 us
  between operations: 14.4 us -> 0.01 us
  starting transfers between devices: 13.3 us -> 0 us
  blocking collectives: 10.4 us -> 0 us
    pallas_call x0 -> x1, Pallas kernels: none -> 64.8 us  [body(): pl.pallas_call(functools.partial(kernel, n, hs, kh, nx), out_shape=jax.Sh...]
    ppermute x7 -> x0, waiting for transfers between devices: 36.7 us -> none  [the longest x3 36.7 us: passed_along(): return lax.ppermute(value, axis, pairs)]
    add x28 -> x0, other arithmetic: 22.6 us -> none  [the longest x8 8.58 us: choose(): picked = picked + jnp.where(wanted == slot_index, candidate, 0.0)]
    unnamed x2 -> x0, waiting for transfers between devices: 21.8 us -> none
    while x63 -> x0, local copies, waits for them, and re-layouts: 17.8 us -> none
    convert_element_type x9 -> x0, other arithmetic: 13.7 us -> none  [the longest x4 6.67 us: add_stop(): direct_radial = stencil(visiting.astype(jnp.float32), 5, radial_cells)]
    ppermute x7 -> x0, starting transfers between devices: 13.3 us -> none  [the longest x2 7.64 us: padded_2(): lax.ppermute(lax.slice_in_dim(block, block.shape[dim] - width, None, axis...]
    div x9 -> x0, other arithmetic: 12.6 us -> none  [stencil(): (shifted(0) - 8.0 * shifted(1) + 8.0 * shifted(3) - shifted(4)) / 12.0]
  transfers between devices with their start and end apart: 8 -> 0, of which waited for: 4 -> 0; matrix products, arithmetic and copies ran while one was open for 31% -> 0% of each run, Pallas kernels for 0% -> 0%
where the time goes in v1:
time: 68.7 us; the launch traced here: 68.5 us
  Pallas kernels  64.8 us (94%)
  local copies, waits for them, and re-layouts  3.63 us (5%)
    pallas_call x1, Pallas kernels, body(): pl.pallas_call(functools.partial(kernel, n, hs, kh, nx), out_shape=jax.Sh...  64.8 us
    unnamed x6, local copies, waits for them, and re-layouts  3.63 us

profile of v1, /device:TPU:0, one launch (start us, length us, event | category | flops | bytes accessed | tf_op | source)
XLA Modules:
  0.0 68.5 jit_solution(4401494091826165059)
XLA Ops:
  0.0 0.8 %copy.4.slots = s32[4,4,2]{2,1,0:T(4,128)S(1)} copy(s32[4,4,2]{1,2,0:T(2,128)} %param.5) | data formatting | bytes 256 | tf_op args[2]
  0.8 0.0 copy-start
  0.8 1.1 %copy-done = bf16[4,4,2,5,16,128]{5,4,3,2,1,0:T(8,128)(2,1)S(1)} copy-done((bf16[4,4,2,5,16,128]{5,4,3,2,1,0:T(8,128)(2,1)S(1)}, bf16[4,4,2,5,16,128]{5,4,3,2,1,0:T(8,128)(2,1)}, u32[]{:S(2)}) %copy-start) | copy-done | bytes 655384
  1.9 0.0 copy-start.1
  1.9 1.1 %copy-done.1 = bf16[4,4,2,5,16,128]{5,4,3,2,1,0:T(8,128)(2,1)S(1)} copy-done((bf16[4,4,2,5,16,128]{5,4,3,2,1,0:T(8,128)(2,1)S(1)}, bf16[4,4,2,5,16,128]{5,4,3,2,1,0:T(8,128)(2,1)}, u32[]{:S(2)}) %copy-start.1) | copy-done | bytes 655384
  3.0 64.8 %shard_map.37 = f32[2,40,4,128]{3,2,1,0:T(4,128)S(1)} custom-call(s32[4,4,2]{2,1,0:T(4,128)S(1)} %copy.4.slots, bf16[2560,128]{1,0:T(8,128)(2,1)S(1)} %bitcast.3, bf16[2560,128]{1,0:T(8,128)(2,1)S(1)} %bitcast.4), custom_call_target="tpu_custom_call" | custom-call | tf_op jit(solution)/shard_map/pallas_call | solution.py:298
  67.8 0.7 copy.6
Async XLA Ops:
  0.8 1.1 %copy-start = (bf16[4,4,2,5,16,128]{5,4,3,2,1,0:T(8,128)(2,1)S(1)}, bf16[4,4,2,5,16,128]{5,4,3,2,1,0:T(8,128)(2,1)}, u32[]{:S(2)}) copy-start(bf16[4,4,2,5,16,128]{5,4,3,2,1,0:T(8,128)(2,1)} %param.3) | copy-start | bytes 1966084
  1.9 1.1 %copy-start.1 = (bf16[4,4,2,5,16,128]{5,4,3,2,1,0:T(8,128)(2,1)S(1)}, bf16[4,4,2,5,16,128]{5,4,3,2,1,0:T(8,128)(2,1)}, u32[]{:S(2)}) copy-start(bf16[4,4,2,5,16,128]{5,4,3,2,1,0:T(8,128)(2,1)} %param.4) | copy-start | bytes 1966084

commit v2 on v1

v2 whole, which is shorter than its diff:
```python
import functools
import math

import jax
import jax.numpy as jnp
from jax import lax
from jax.experimental import pallas as pl
from jax.experimental.pallas import tpu as pltpu
from jax.sharding import PartitionSpec as P

HARMS = 8
SLOTS = 4
FIELDS = 5
PLANES = 2 * FIELDS
MESH = pl.DeviceIdType.MESH


def coefficient(offset):
    value = jnp.where(offset == 1, 8.0, 0.0)
    value = jnp.where(offset == -1, -8.0, value)
    value = jnp.where(offset == 2, -1.0, value)
    value = jnp.where(offset == -2, 1.0, value)
    return value


def kernel(
    n, hs, kh, nx,
    slots, d_hbm, a_hbm, out_ref,
    gbuf, pbuf, abuf, apbuf, ebuf, epbuf,
    d_st, dx_st, dr_st, a_st, ax_st, ar_st, e_st, ex_st, er_st,
    run, run_e, sbuf, sbuf_e, rbuf, rbuf_e, radial, axial, slots_e,
    local_d, local_a,
    right_send, right_recv, left_send, left_recv,
    core_send, core_recv, adj_send, adj_recv,
    edge_send, edge_recv, edge_core_send, edge_core_recv, slots_sem,
    slab_send, slab_recv, slab_send_e, slab_recv_e,
):
    me = lax.axis_index("mode")
    my_harm = lax.axis_index("harm")
    core = lax.axis_index("rad")
    per_owner = n // hs
    cells = nx // n
    rows = d_hbm.shape[1]
    chunk = axial.shape[0]
    planes_k = SLOTS * PLANES
    first, last = me == 0, me == n - 1
    low_helper, high_helper = me == 1, me == n - 2

    for k in range(kh):
        pltpu.make_async_copy(d_hbm.at[k], gbuf.at[me, k], local_d.at[k]).start()
    for k in range(kh):
        pltpu.make_async_copy(a_hbm.at[k], abuf.at[k], local_a.at[k]).start()

    barrier = pltpu.get_barrier_semaphore()

    def greet(index, carry):
        q = index // hs
        h = index % hs

        @pl.when(jnp.logical_or(q != me, h != my_harm))
        def _():
            pl.semaphore_signal(barrier, inc=1, device_id={"mode": q, "harm": h}, device_id_type=MESH)

        return carry

    lax.fori_loop(0, n * hs, greet, 0)
    pl.semaphore_signal(barrier, inc=1, device_id={"rad": 1 - core}, device_id_type=MESH)

    row = lax.broadcasted_iota(jnp.int32, (128, 128), 0)
    col = lax.broadcasted_iota(jnp.int32, (128, 128), 1)
    shift = (1 - 2 * core) * 128
    radial[0:128, :] = coefficient(row - col).astype(jnp.bfloat16)
    radial[128:256, :] = coefficient(row - col + shift).astype(jnp.bfloat16)
    row = lax.broadcasted_iota(jnp.int32, (chunk, chunk), 0)
    col = lax.broadcasted_iota(jnp.int32, (chunk, chunk), 1)
    same = (row // nx) == (col // nx)
    axial[...] = jnp.where(same, coefficient(col - row), 0.0).astype(jnp.bfloat16)
    run[...] = jnp.zeros_like(run)
    run_e[...] = jnp.zeros_like(run_e)

    pl.semaphore_wait(barrier, n * hs)

    def remote(src, dst, send, recv, target):
        return pltpu.make_async_remote_copy(
            src_ref=src, dst_ref=dst, send_sem=send, recv_sem=recv,
            device_id=target, device_id_type=MESH)

    other = {"rad": 1 - core}

    def to_right(block, k):
        return remote(gbuf.at[block, k], gbuf.at[block, k],
                      right_send.at[block, k], right_recv.at[block, k], {"mode": me + 1})

    def to_left(block, k):
        return remote(gbuf.at[block, k], gbuf.at[block, k],
                      left_send.at[block, k], left_recv.at[block, k], {"mode": me - 1})

    def to_core(block, k):
        return remote(gbuf.at[block, k], pbuf.at[block, k],
                      core_send.at[block, k], core_recv.at[block, k], other)

    def adjoint_to_core(k):
        return remote(abuf.at[k], apbuf.at[k], adj_send.at[k], adj_recv.at[k], other)

    def edge(k, target):
        return remote(abuf.at[k], ebuf.at[k], edge_send.at[k], edge_recv.at[k], {"mode": target})

    def edge_to_core(k):
        return remote(ebuf.at[k], epbuf.at[k], edge_core_send.at[k], edge_core_recv.at[k], other)

    def edge_slots(target):
        return remote(slots, slots_e, slots_sem.at[0], slots_sem.at[1], {"mode": target})

    for k in range(kh):
        pltpu.make_async_copy(d_hbm.at[k], gbuf.at[me, k], local_d.at[k]).wait()

        @pl.when(me < n - 1)
        def _():
            to_right(me, k).start()

        @pl.when(me > 0)
        def _():
            to_left(me, k).start()

        to_core(me, k).start()

    for k in range(kh):
        pltpu.make_async_copy(a_hbm.at[k], abuf.at[k], local_a.at[k]).wait()
        adjoint_to_core(k).start()

    @pl.when(first)
    def _():
        edge_slots(1).start()

    @pl.when(last)
    def _():
        edge_slots(n - 2).start()

    def prepare(own, partner, plain, along_x, along_r, base):
        def step(i, carry):
            at = pl.ds(pl.multiple_of(i * chunk, chunk), chunk)
            planes = pl.ds(base + i * (chunk // nx), chunk // nx)
            mine = own[at, :]
            both = jnp.concatenate([mine, partner[at, :]], axis=1)
            shape = (chunk // nx, nx, 128)
            plain[planes] = mine.astype(jnp.float32).reshape(shape)
            along_r[planes] = jnp.dot(
                both, radial[...], preferred_element_type=jnp.float32).reshape(shape)
            along_x[planes] = jnp.dot(
                axial[...], mine, preferred_element_type=jnp.float32).reshape(shape)
            return carry

        lax.fori_loop(0, rows // chunk, step, 0)

    def products(table, stop, total, adj, adj_x, adj_r, base):
        def one_mode(m, carry):
            da = base + table[m, stop, 0] * PLANES
            dd = table[m, stop, 1] * PLANES
            for half in range(nx // 8):
                part = pl.ds(half * 8, 8)
                d1r = d_st[dd + 1, part, :]
                d2r = d_st[dd + 2, part, :]
                d1i = d_st[dd + FIELDS + 1, part, :]
                d2i = d_st[dd + FIELDS + 2, part, :]
                a1r = adj[da + 1, part, :]
                a2r = adj[da + 2, part, :]
                a1i = adj[da + FIELDS + 1, part, :]
                a2i = adj[da + FIELDS + 2, part, :]
                for f in range(FIELDS):
                    axr = adj_x[da + f, part, :]
                    axi = adj_x[da + FIELDS + f, part, :]
                    arr = adj_r[da + f, part, :]
                    ari = adj_r[da + FIELDS + f, part, :]
                    dxr = dx_st[dd + f, part, :]
                    dxi = dx_st[dd + FIELDS + f, part, :]
                    drr = dr_st[dd + f, part, :]
                    dri = dr_st[dd + FIELDS + f, part, :]
                    total[m * PLANES + f, part, :] += (
                        ((d1r * axr + d1i * axi) + (d2r * arr + d2i * ari))
                        + ((dxr * a1r + dxi * a1i) + (drr * a2r + dri * a2i)))
                    total[m * PLANES + FIELDS + f, part, :] += (
                        ((d1r * axi - d1i * axr) + (d2r * ari - d2i * arr))
                        + ((dxr * a1i - dxi * a1r) + (drr * a2i - dri * a2r)))
            return carry

        lax.fori_loop(0, SLOTS, one_mode, 0)

    def visit(block, stop, k):
        to_core(block, k).wait_recv()
        prepare(gbuf.at[block, k], pbuf.at[block, k], d_st, dx_st, dr_st, 0)
        products(slots, stop, run, a_st, ax_st, ar_st, k * planes_k)

    def visit_edge(stop, k):
        edge_to_core(k).wait_recv()
        prepare(ebuf.at[k], epbuf.at[k], e_st, ex_st, er_st, 0)
        products(slots_e, stop, run_e, e_st, ex_st, er_st, 0)

    def arrive_chunk(hop, k):
        from_left = me - hop
        from_right = me + hop

        @pl.when(from_left >= 0)
        def _():
            to_right(from_left, k).wait_recv()

            @pl.when(jnp.logical_and(me < n - 1, jnp.logical_or(me < n - 2, from_left > 0)))
            def _():
                to_right(from_left, k).start()

            to_core(from_left, k).start()

        @pl.when(from_right < n)
        def _():
            to_left(from_right, k).wait_recv()

            @pl.when(jnp.logical_and(me > 0, jnp.logical_or(me > 1, from_right < n - 1)))
            def _():
                to_left(from_right, k).start()

            to_core(from_right, k).start()

        @pl.when(jnp.logical_and(hop == 1, first))
        def _():
            to_right(me, k).wait_send()
            edge(k, 1).start()

        @pl.when(jnp.logical_and(hop == 1, last))
        def _():
            to_left(me, k).wait_send()
            edge(k, n - 2).start()

        @pl.when(jnp.logical_and(hop == n - 2, jnp.logical_or(low_helper, high_helper)))
        def _():
            edge(k, me).wait_recv()
            edge_to_core(k).start()

    def visit_chunk(hop, k):
        @pl.when(me - hop >= 0)
        def _():
            visit(me - hop, hop, k)

            @pl.when(jnp.logical_and(hop == n - 2, high_helper))
            def _():
                visit_edge(n - 1, k)

        @pl.when(me + hop < n)
        def _():
            visit(me + hop, n - hop, k)

            @pl.when(jnp.logical_and(hop == n - 2, low_helper))
            def _():
                visit_edge(1, k)

    def own_chunk(k, carry):
        adjoint_to_core(k).wait_recv()
        prepare(abuf.at[k], apbuf.at[k], a_st, ax_st, ar_st, k * planes_k)
        visit(me, 0, k)
        return carry

    lax.fori_loop(0, kh, own_chunk, 0)

    @pl.when(jnp.logical_or(low_helper, high_helper))
    def _():
        edge_slots(me).wait_recv()

    count = (n - 2) * kh

    def steps(i, carry):
        @pl.when(i < count)
        def _():
            arrive_chunk(1 + i // kh, i % kh)

        @pl.when(i > 0)
        def _():
            visit_chunk(1 + (i - 1) // kh, (i - 1) % kh)

        return carry

    lax.fori_loop(0, count + 1, steps, 0)

    scale = 1.0 / (12.0 * math.sqrt(8.0 * n * HARMS))
    owner = me // per_owner
    place = me % per_owner
    helper = jnp.logical_or(low_helper, high_helper)
    side = jnp.where(low_helper, 0, 1)
    owner_e = jnp.where(low_helper, 0, hs - 1)

    def slab(q, h, i):
        return remote(sbuf.at[q], rbuf.at[h * per_owner + i],
                      slab_send.at[q], slab_recv.at[h * per_owner + i],
                      {"mode": q, "harm": owner})

    def slab_e(q, h, i):
        return remote(sbuf_e.at[q], rbuf_e.at[i * hs + h],
                      slab_send_e.at[q], slab_recv_e.at[i * hs + h],
                      {"mode": q, "harm": owner_e})

    def each_target(act, act_e):
        def step(q, carry):
            @pl.when(jnp.logical_or(q != me, owner != my_harm))
            def _():
                act(slab(q, my_harm, place))

            @pl.when(jnp.logical_and(helper, jnp.logical_or(q != me, owner_e != my_harm)))
            def _():
                act_e(slab_e(q, my_harm, side))

            return carry

        lax.fori_loop(0, n, step, 0)

    for q in range(n):
        sbuf[q] = run[:, q * cells:(q + 1) * cells, :] * scale

    @pl.when(helper)
    def _():
        for q in range(n):
            sbuf_e[q] = run_e[:, q * cells:(q + 1) * cells, :] * scale

    each_target(lambda copy: copy.start(), lambda copy: copy.start())

    @pl.when(owner == my_harm)
    def _():
        rbuf[my_harm * per_owner + place] = sbuf[me]

    @pl.when(jnp.logical_and(helper, owner_e == my_harm))
    def _():
        rbuf_e[side * hs + my_harm] = sbuf_e[me]

    def arrive(index, carry):
        h = index // per_owner
        i = index % per_owner
        mine = jnp.logical_and(h == my_harm, my_harm * per_owner + i == me)

        @pl.when(jnp.logical_not(mine))
        def _():
            slab(0, h, i).wait_recv()

        return carry

    lax.fori_loop(0, hs * per_owner, arrive, 0)
    for i in range(per_owner):
        total = rbuf[i]
        for h in range(1, hs):
            total = total + rbuf[h * per_owner + i]
        out_ref[i] = total

    for i, source, holder, spot in ((0, 1, 0, 0), (1, n - 2, hs - 1, per_owner - 1)):
        @pl.when(my_harm == holder)
        def _(i=i, source=source, spot=spot):
            def wait_edge(h, carry):
                @pl.when(jnp.logical_or(h != my_harm, me != source))
                def _():
                    slab_e(0, h, i).wait_recv()

                return carry

            lax.fori_loop(0, hs, wait_edge, 0)
            total = out_ref[spot]
            for h in range(hs):
                total = total + rbuf_e[i * hs + h]
            out_ref[spot] = total

    each_target(lambda copy: copy.wait_send(), lambda copy: copy.wait_send())

    def drain(i, carry):
        block = i // kh
        k = i % kh

        @pl.when(jnp.logical_not(jnp.logical_or(
            jnp.logical_and(first, block == n - 1), jnp.logical_and(last, block == 0))))
        def _():
            to_core(block, k).wait_send()

        @pl.when(jnp.logical_and(
            jnp.logical_and(block <= me, me < n - 1),
            jnp.logical_and(
                jnp.logical_or(me < n - 2, block > 0),
                jnp.logical_not(first))))
        def _():
            to_right(block, k).wait_send()

        @pl.when(jnp.logical_and(
            jnp.logical_and(block >= me, me > 0),
            jnp.logical_and(
                jnp.logical_or(me > 1, block < n - 1),
                jnp.logical_not(last))))
        def _():
            to_left(block, k).wait_send()

        return carry

    lax.fori_loop(0, n * kh, drain, 0)

    def drain_adjoint(k, carry):
        adjoint_to_core(k).wait_send()

        @pl.when(jnp.logical_or(first, last))
        def _():
            edge(k, me).wait_send()

        @pl.when(helper)
        def _():
            edge_to_core(k).wait_send()

        return carry

    lax.fori_loop(0, kh, drain_adjoint, 0)

    @pl.when(jnp.logical_or(first, last))
    def _():
        edge_slots(me).wait_send()


def body(hs, direct_field, adjoint_field, triad_slots):
    n = triad_slots.shape[1]
    kh = direct_field.shape[0]
    nx = direct_field.shape[4]
    planes = SLOTS * PLANES
    rows = planes * nx
    chunk = 128
    cells = nx // n
    per_owner = n // hs
    f32, bf16 = jnp.float32, jnp.bfloat16
    dma = pltpu.SemaphoreType.DMA
    slab_shape = (planes, cells, 128)
    out = pl.pallas_call(
        functools.partial(kernel, n, hs, kh, nx),
        out_shape=jax.ShapeDtypeStruct((per_owner,) + slab_shape, f32),
        in_specs=[pl.BlockSpec(memory_space=pltpu.SMEM)] + [pl.BlockSpec(memory_space=pl.ANY)] * 2,
        out_specs=pl.BlockSpec(memory_space=pltpu.VMEM),
        scratch_shapes=[pltpu.VMEM((n, kh, rows, 128), bf16)] * 2
        + [pltpu.VMEM((kh, rows, 128), bf16)] * 4
        + [pltpu.VMEM((planes, nx, 128), f32)] * 3
        + [pltpu.VMEM((kh * planes, nx, 128), f32)] * 3
        + [pltpu.VMEM((planes, nx, 128), f32)] * 5
        + [
            pltpu.VMEM((n,) + slab_shape, f32),
            pltpu.VMEM((n,) + slab_shape, f32),
            pltpu.VMEM((hs * per_owner,) + slab_shape, f32),
            pltpu.VMEM((2 * hs,) + slab_shape, f32),
            pltpu.VMEM((256, 128), bf16),
            pltpu.VMEM((chunk, chunk), bf16),
            pltpu.SMEM(triad_slots.shape, jnp.int32),
            dma((kh,)), dma((kh,)),
            dma((n, kh)), dma((n, kh)), dma((n, kh)), dma((n, kh)),
            dma((n, kh)), dma((n, kh)), dma((kh,)), dma((kh,)),
            dma((kh,)), dma((kh,)), dma((kh,)), dma((kh,)), dma((2,)),
            dma((n,)), dma((hs * per_owner,)), dma((n,)), dma((2 * hs,)),
        ],
        compiler_params=pltpu.CompilerParams(
            collective_id=0, has_side_effects=True, vmem_limit_bytes=56 << 20),
    )(
        triad_slots,
        direct_field.reshape(kh, rows, 128),
        adjoint_field.reshape(kh, rows, 128),
    )
    return out.reshape(per_owner * SLOTS, 2, FIELDS, cells, 128)


def solution(mesh):
    return jax.shard_map(
        functools.partial(body, mesh.shape["harm"]),
        mesh=mesh,
        in_specs=(
            P(("case", "harm"), "mode", None, None, None, "rad"),
            P(("case", "harm"), "mode", None, None, None, "rad"),
            P("mode", None, None),
        ),
        out_specs=P(("case", "harm"), None, None, "mode", "rad"),
        check_vma=False,
    )
```

time: 68.7 us -> 57.6 us (0.84)
  Pallas kernels: 64.8 us -> 54.1 us
    pallas_call x1, Pallas kernels: 64.8 us -> 54.1 us  [body(): pl.pallas_call(functools.partial(kernel, n, hs, kh, nx), out_shape=jax.Sh...]
    unnamed x6 -> x2, local copies, waits for them, and re-layouts: 3.63 us -> 2.98 us
where the time goes in v2:
time: 57.6 us; the launch traced here: 57.1 us
  Pallas kernels  54.1 us (94%)
  local copies, waits for them, and re-layouts  2.98 us (5%)
    pallas_call x1, Pallas kernels, body(): pl.pallas_call(functools.partial(kernel, n, hs, kh, nx), out_shape=jax.Sh...  54.1 us
    unnamed x2, local copies, waits for them, and re-layouts  2.98 us

profile of v2, /device:TPU:0, one launch (start us, length us, event | category | flops | bytes accessed | tf_op | source)
XLA Modules:
  0.0 57.1 jit_solution(11324527658647752259)
XLA Ops:
  0.0 1.4 %copy.4.slots = s32[4,4,2]{2,1,0:T(4,128)} copy(s32[4,4,2]{1,2,0:T(2,128)} %param.5) | data formatting | bytes 256 | tf_op args[2]
  1.4 54.1 %shard_map.37 = f32[2,40,4,128]{3,2,1,0:T(4,128)} custom-call(s32[4,4,2]{2,1,0:T(4,128)} %copy.4.slots, bf16[4,640,128]{2,1,0:T(8,128)(2,1)} %bitcast.3, bf16[4,640,128]{2,1,0:T(8,128)(2,1)} %bitcast.4), custom_call_target="tpu_custom_call" | custom-call | tf_op jit(solution)/shard_map/pallas_call | solution.py:427
  55.5 1.6 %copy.6 = f32[8,2,5,4,128]{4,3,2,1,0:T(4,128)} copy(f32[8,2,5,4,128]{4,3,2,1,0:T(4,128)} %bitcast.5) | data formatting | bytes 327680

commit v3 on v2

--- a/solution.py
+++ b/solution.py
@@ -154,8 +154,8 @@
 
     def products(table, stop, total, adj, adj_x, adj_r, base):
         def one_mode(m, carry):
-            da = base + table[m, stop, 0] * PLANES
-            dd = table[m, stop, 1] * PLANES
+            da = base + table[m, 0, stop] * PLANES
+            dd = table[m, 1, stop] * PLANES
             for half in range(nx // 8):
                 part = pl.ds(half * 8, 8)
                 d1r = d_st[dd + 1, part, :]
@@ -427,7 +427,7 @@
     out = pl.pallas_call(
         functools.partial(kernel, n, hs, kh, nx),
         out_shape=jax.ShapeDtypeStruct((per_owner,) + slab_shape, f32),
-        in_specs=[pl.BlockSpec(memory_space=pltpu.SMEM)] + [pl.BlockSpec(memory_space=pl.ANY)] * 2,
+        in_specs=[pl.BlockSpec(memory_space=pltpu.SMEM)] + [pl.BlockSpec(memory_space=pltpu.HBM)] * 2,
         out_specs=pl.BlockSpec(memory_space=pltpu.VMEM),
         scratch_shapes=[pltpu.VMEM((n, kh, rows, 128), bf16)] * 2
         + [pltpu.VMEM((kh, rows, 128), bf16)] * 4
@@ -441,7 +441,7 @@
             pltpu.VMEM((2 * hs,) + slab_shape, f32),
             pltpu.VMEM((256, 128), bf16),
             pltpu.VMEM((chunk, chunk), bf16),
-            pltpu.SMEM(triad_slots.shape, jnp.int32),
+            pltpu.SMEM((SLOTS, 2, n), jnp.int32),
             dma((kh,)), dma((kh,)),
             dma((n, kh)), dma((n, kh)), dma((n, kh)), dma((n, kh)),
             dma((n, kh)), dma((n, kh)), dma((kh,)), dma((kh,)),
@@ -449,9 +449,9 @@
             dma((n,)), dma((hs * per_owner,)), dma((n,)), dma((2 * hs,)),
         ],
         compiler_params=pltpu.CompilerParams(
-            collective_id=0, has_side_effects=True, vmem_limit_bytes=56 << 20),
+            collective_id=0, has_side_effects=True, vmem_limit_bytes=56_000_000),
     )(
-        triad_slots,
+        jnp.transpose(triad_slots, (0, 2, 1)),
         direct_field.reshape(kh, rows, 128),
         adjoint_field.reshape(kh, rows, 128),
     )

time: 57.6 us -> 55.1 us (0.957)
  local copies, waits for them, and re-layouts: 2.98 us -> 1.36 us
  Pallas kernels: 54.1 us -> 53.2 us
    unnamed x2 -> x3, local copies, waits for them, and re-layouts: 2.98 us -> 1.36 us
    pallas_call x1, Pallas kernels: 54.1 us -> 53.2 us  [body(): pl.pallas_call(functools.partial(kernel, n, hs, kh, nx), out_shape=jax.Sh...]
where the time goes in v3:
time: 55.1 us; the launch traced here: 54.6 us
  Pallas kernels  53.2 us (97%)
  local copies, waits for them, and re-layouts  1.36 us (2%)
    pallas_call x1, Pallas kernels, body(): pl.pallas_call(functools.partial(kernel, n, hs, kh, nx), out_shape=jax.Sh...  53.2 us
    unnamed x3, local copies, waits for them, and re-layouts  1.36 us

profile of v3, /device:TPU:0, one launch (start us, length us, event | category | flops | bytes accessed | tf_op | source)
XLA Modules:
  0.0 54.6 jit_solution(5465957970521352917)
XLA Ops:
  0.0 0.0 copy-start
  0.0 0.7 %copy-done = s32[4,4,2]{1,2,0:T(2,128)S(1)} copy-done((s32[4,4,2]{1,2,0:T(2,128)S(1)}, s32[4,4,2]{1,2,0:T(2,128)}, u32[]{:S(2)}) %copy-start) | copy-done | bytes 152
  0.7 53.2 %shard_map.37 = f32[2,40,4,128]{3,2,1,0:T(4,128)S(1)} custom-call(s32[4,2,4]{2,1,0:T(2,128)S(1)} %bitcast.5, bf16[4,640,128]{2,1,0:T(8,128)(2,1)} %bitcast.6, bf16[4,640,128]{2,1,0:T(8,128)(2,1)} %bitcast.7), custom_call_target="tpu_custom_call" | custom-call | tf_op jit(solution)/shard_map/pallas_call | solution.py:427
  53.9 0.7 %copy.5 = f32[8,2,5,4,128]{4,3,2,1,0:T(4,128)} copy(f32[8,2,5,4,128]{4,3,2,1,0:T(4,128)S(1)} %bitcast.4) | data formatting | bytes 327680
Async XLA Ops:
  0.0 0.7 %copy-start = (s32[4,4,2]{1,2,0:T(2,128)S(1)}, s32[4,4,2]{1,2,0:T(2,128)}, u32[]{:S(2)}) copy-start(s32[4,4,2]{1,2,0:T(2,128)} %param.5) | copy-start | bytes 388

commit v4 on v3

v4 whole, which is shorter than its diff:
```python
import functools
import math

import jax
import jax.numpy as jnp
from jax import lax
from jax.experimental import pallas as pl
from jax.experimental.pallas import tpu as pltpu
from jax.sharding import PartitionSpec as P

HARMS = 8
SLOTS = 4
FIELDS = 5
ORDER = (1, 2, 0, 3, 4)
MESH = pl.DeviceIdType.MESH


def coefficient(offset):
    value = jnp.where(offset == 1, 8.0, 0.0)
    value = jnp.where(offset == -1, -8.0, value)
    value = jnp.where(offset == 2, -1.0, value)
    value = jnp.where(offset == -2, 1.0, value)
    return value


def kernel(
    n, hs, kh, nx,
    slots, d_hbm, a_hbm, out_ref,
    gbuf, pbuf, abuf, apbuf, ebuf, epbuf,
    d_st, dx_st, dr_st, f_st, fx_st, fr_st, a_st, ax_st, ar_st, e_st, ex_st, er_st,
    run, run_e, sbuf, sbuf_e, rbuf, rbuf_e, radial, axial, slots_e,
    local_d, local_a,
    right_send, right_recv, left_send, left_recv,
    core_send, core_recv, adj_send, adj_recv,
    edge_send, edge_recv, edge_core_send, edge_core_recv, slots_sem,
    slab_send, slab_recv, slab_send_e, slab_recv_e,
):
    me = lax.axis_index("mode")
    my_harm = lax.axis_index("harm")
    core = lax.axis_index("rad")
    per_owner = n // hs
    cells = nx // n
    wide = d_hbm.shape[0]
    chunk = axial.shape[0]
    first, last = me == 0, me == n - 1
    low_helper, high_helper = me == 1, me == n - 2

    for k in range(FIELDS):
        pltpu.make_async_copy(d_hbm.at[:, ORDER[k]], gbuf.at[me, k], local_d.at[k]).start()
    for k in range(FIELDS):
        pltpu.make_async_copy(a_hbm.at[:, ORDER[k]], abuf.at[k], local_a.at[k]).start()

    barrier = pltpu.get_barrier_semaphore()

    def greet(index, carry):
        q = index // hs
        h = index % hs

        @pl.when(jnp.logical_or(q != me, h != my_harm))
        def _():
            pl.semaphore_signal(barrier, inc=1, device_id={"mode": q, "harm": h}, device_id_type=MESH)

        return carry

    lax.fori_loop(0, n * hs, greet, 0)
    pl.semaphore_signal(barrier, inc=1, device_id={"rad": 1 - core}, device_id_type=MESH)

    row = lax.broadcasted_iota(jnp.int32, (128, 128), 0)
    col = lax.broadcasted_iota(jnp.int32, (128, 128), 1)
    shift = (1 - 2 * core) * 128
    radial[0:128, :] = coefficient(row - col).astype(jnp.bfloat16)
    radial[128:256, :] = coefficient(row - col + shift).astype(jnp.bfloat16)
    row = lax.broadcasted_iota(jnp.int32, (chunk, chunk), 0)
    col = lax.broadcasted_iota(jnp.int32, (chunk, chunk), 1)
    same = (row // nx) == (col // nx)
    axial[...] = jnp.where(same, coefficient(col - row), 0.0).astype(jnp.bfloat16)
    run[...] = jnp.zeros_like(run)
    run_e[...] = jnp.zeros_like(run_e)

    pl.semaphore_wait(barrier, n * hs)

    def remote(src, dst, send, recv, target):
        return pltpu.make_async_remote_copy(
            src_ref=src, dst_ref=dst, send_sem=send, recv_sem=recv,
            device_id=target, device_id_type=MESH)

    other = {"rad": 1 - core}

    def to_right(block, k):
        return remote(gbuf.at[block, k], gbuf.at[block, k],
                      right_send.at[block, k], right_recv.at[block, k], {"mode": me + 1})

    def to_left(block, k):
        return remote(gbuf.at[block, k], gbuf.at[block, k],
                      left_send.at[block, k], left_recv.at[block, k], {"mode": me - 1})

    def to_core(block, k):
        return remote(gbuf.at[block, k], pbuf.at[block, k],
                      core_send.at[block, k], core_recv.at[block, k], other)

    def adjoint_to_core(k):
        return remote(abuf.at[k], apbuf.at[k], adj_send.at[k], adj_recv.at[k], other)

    def edge(k, target):
        return remote(abuf.at[k], ebuf.at[k], edge_send.at[k], edge_recv.at[k], {"mode": target})

    def edge_to_core(k):
        return remote(ebuf.at[k], epbuf.at[k], edge_core_send.at[k], edge_core_recv.at[k], other)

    def edge_slots(target):
        return remote(slots, slots_e, slots_sem.at[0], slots_sem.at[1], {"mode": target})

    for k in range(FIELDS):
        pltpu.make_async_copy(d_hbm.at[:, ORDER[k]], gbuf.at[me, k], local_d.at[k]).wait()

        @pl.when(me < n - 1)
        def _():
            to_right(me, k).start()

        @pl.when(me > 0)
        def _():
            to_left(me, k).start()

        to_core(me, k).start()

    for k in range(FIELDS):
        pltpu.make_async_copy(a_hbm.at[:, ORDER[k]], abuf.at[k], local_a.at[k]).wait()
        adjoint_to_core(k).start()

    @pl.when(first)
    def _():
        edge_slots(1).start()

    @pl.when(last)
    def _():
        edge_slots(n - 2).start()

    def prepare(own, partner, plain, along_x, along_r, k):
        group = chunk // nx

        def step(i, carry):
            at = pl.ds(i * group, group)
            to = pl.ds(k * wide + i * group, group)
            mine = own[at].reshape(chunk, 128)
            both = jnp.concatenate([mine, partner[at].reshape(chunk, 128)], axis=1)
            shape = (group, nx, 128)

            @pl.when(k < 2)
            def _():
                plain[to] = mine.astype(jnp.float32).reshape(shape)

            along_r[to] = jnp.dot(
                both, radial[...], preferred_element_type=jnp.float32).reshape(shape)
            along_x[to] = jnp.dot(
                axial[...], mine, preferred_element_type=jnp.float32).reshape(shape)
            return carry

        lax.fori_loop(0, wide // group, step, 0)

    def products(table, stop, total, dirs, adjs, k):
        d_pl, d_x, d_r = dirs
        a_pl, a_x, a_r = adjs

        def one_mode(m, carry):
            da = table[m, 0, stop] * 2
            dd = table[m, 1, stop] * 2
            for half in range(nx // 8):
                part = pl.ds(half * 8, 8)
                real = total[(k * SLOTS + m) * 2, part, :]
                imag = total[(k * SLOTS + m) * 2 + 1, part, :]
                for c in range(kh):
                    ia = c * SLOTS * 2 + da
                    id_ = c * SLOTS * 2 + dd
                    d1r = d_pl[id_, part, :]
                    d1i = d_pl[id_ + 1, part, :]
                    d2r = d_pl[wide + id_, part, :]
                    d2i = d_pl[wide + id_ + 1, part, :]
                    a1r = a_pl[ia, part, :]
                    a1i = a_pl[ia + 1, part, :]
                    a2r = a_pl[wide + ia, part, :]
                    a2i = a_pl[wide + ia + 1, part, :]
                    axr = a_x[k * wide + ia, part, :]
                    axi = a_x[k * wide + ia + 1, part, :]
                    arr = a_r[k * wide + ia, part, :]
                    ari = a_r[k * wide + ia + 1, part, :]
                    dxr = d_x[k * wide + id_, part, :]
                    dxi = d_x[k * wide + id_ + 1, part, :]
                    drr = d_r[k * wide + id_, part, :]
                    dri = d_r[k * wide + id_ + 1, part, :]
                    real = real + (
                        ((d1r * axr + d1i * axi) + (d2r * arr + d2i * ari))
                        + ((dxr * a1r + dxi * a1i) + (drr * a2r + dri * a2i)))
                    imag = imag + (
                        ((d1r * axi - d1i * axr) + (d2r * ari - d2i * arr))
                        + ((dxr * a1i - dxi * a1r) + (drr * a2i - dri * a2r)))
                total[(k * SLOTS + m) * 2, part, :] = real
                total[(k * SLOTS + m) * 2 + 1, part, :] = imag
            return carry

        lax.fori_loop(0, SLOTS, one_mode, 0)

    def ready(k, act):
        def step(c, carry):
            act(c)
            return carry

        low = jnp.where(k == 0, 1, jnp.where(k == 1, 0, k))
        lax.fori_loop(low, k + 1, step, 0)

    left_side = (d_st, dx_st, dr_st)
    right_side = (f_st, fx_st, fr_st)
    own_adjoint = (a_st, ax_st, ar_st)
    edge_adjoint = (e_st, ex_st, er_st)

    def visit(block, stop, k, side):
        to_core(block, k).wait_recv()
        prepare(gbuf.at[block, k], pbuf.at[block, k], *side, k)
        ready(k, lambda c: products(slots, stop, run, side, own_adjoint, c))

    def visit_edge(stop, k, side):
        edge_to_core(k).wait_recv()
        prepare(ebuf.at[k], epbuf.at[k], *edge_adjoint, k)
        ready(k, lambda c: products(slots_e, stop, run_e, side, edge_adjoint, c))

    def arrive_chunk(hop, k):
        from_left = me - hop
        from_right = me + hop

        @pl.when(from_left >= 0)
        def _():
            to_right(from_left, k).wait_recv()

            @pl.when(jnp.logical_and(me < n - 1, jnp.logical_or(me < n - 2, from_left > 0)))
            def _():
                to_right(from_left, k).start()

            to_core(from_left, k).start()

        @pl.when(from_right < n)
        def _():
            to_left(from_right, k).wait_recv()

            @pl.when(jnp.logical_and(me > 0, jnp.logical_or(me > 1, from_right < n - 1)))
            def _():
                to_left(from_right, k).start()

            to_core(from_right, k).start()

        @pl.when(jnp.logical_and(hop == 1, first))
        def _():
            to_right(me, k).wait_send()
            edge(k, 1).start()

        @pl.when(jnp.logical_and(hop == 1, last))
        def _():
            to_left(me, k).wait_send()
            edge(k, n - 2).start()

        @pl.when(jnp.logical_and(hop == n - 2, jnp.logical_or(low_helper, high_helper)))
        def _():
            edge(k, me).wait_recv()
            edge_to_core(k).start()

    def visit_chunk(hop, k):
        @pl.when(me - hop >= 0)
        def _():
            visit(me - hop, hop, k, left_side)

            @pl.when(jnp.logical_and(hop == n - 2, high_helper))
            def _():
                visit_edge(n - 1, k, left_side)

        @pl.when(me + hop < n)
        def _():
            visit(me + hop, n - hop, k, right_side)

            @pl.when(jnp.logical_and(hop == n - 2, low_helper))
            def _():
                visit_edge(1, k, right_side)

    scale = 1.0 / (12.0 * math.sqrt(8.0 * n * HARMS))
    owner = me // per_owner
    place = me % per_owner
    helper = jnp.logical_or(low_helper, high_helper)
    side = jnp.where(low_helper, 0, 1)
    owner_e = jnp.where(low_helper, 0, hs - 1)

    def slab(k, q, h, i):
        return remote(sbuf.at[k, q], rbuf.at[k, h * per_owner + i],
                      slab_send.at[k, q], slab_recv.at[k, h * per_owner + i],
                      {"mode": q, "harm": owner})

    def slab_e(k, q, h, i):
        return remote(sbuf_e.at[k, q], rbuf_e.at[k, i * hs + h],
                      slab_send_e.at[k, q], slab_recv_e.at[k, i * hs + h],
                      {"mode": q, "harm": owner_e})

    def each_target(k, act):
        def step(q, carry):
            @pl.when(jnp.logical_or(q != me, owner != my_harm))
            def _():
                act(slab(k, q, my_harm, place))

            @pl.when(jnp.logical_and(helper, jnp.logical_or(q != me, owner_e != my_harm)))
            def _():
                act(slab_e(k, q, my_harm, side))

            return carry

        lax.fori_loop(0, n, step, 0)

    def deliver(k):
        span = pl.ds(k * SLOTS * 2, SLOTS * 2)
        for q in range(n):
            sbuf[k, q] = run[span, q * cells:(q + 1) * cells, :] * scale

        @pl.when(helper)
        def _():
            for q in range(n):
                sbuf_e[k, q] = run_e[span, q * cells:(q + 1) * cells, :] * scale

        each_target(k, lambda copy: copy.start())

        @pl.when(owner == my_harm)
        def _():
            rbuf[k, my_harm * per_owner + place] = sbuf[k, me]

        @pl.when(jnp.logical_and(helper, owner_e == my_harm))
        def _():
            rbuf_e[k, side * hs + my_harm] = sbuf_e[k, me]

    def own_chunk(k, carry):
        adjoint_to_core(k).wait_recv()
        prepare(abuf.at[k], apbuf.at[k], *own_adjoint, k)
        visit(me, 0, k, left_side)
        return carry

    lax.fori_loop(0, FIELDS, own_chunk, 0)

    @pl.when(jnp.logical_or(low_helper, high_helper))
    def _():
        edge_slots(me).wait_recv()

    count = (n - 2) * FIELDS

    def steps(i, carry):
        @pl.when(i < count)
        def _():
            arrive_chunk(1 + i // FIELDS, i % FIELDS)

        @pl.when(i > 0)
        def _():
            visit_chunk(1 + (i - 1) // FIELDS, (i - 1) % FIELDS)

        @pl.when(i > count - FIELDS)
        def _():
            ready(i - 1 - (count - FIELDS), deliver)

        return carry

    lax.fori_loop(0, count + 1, steps, 0)

    def collect(k, carry):
        def arrive(index, inner):
            h = index // per_owner
            i = index % per_owner
            mine = jnp.logical_and(h == my_harm, my_harm * per_owner + i == me)

            @pl.when(jnp.logical_not(mine))
            def _():
                slab(k, 0, h, i).wait_recv()

            return inner

        lax.fori_loop(0, hs * per_owner, arrive, 0)
        field = jnp.where(k < 2, k + 1, jnp.where(k == 2, 0, k))
        for i in range(per_owner):
            total = rbuf[k, i]
            for h in range(1, hs):
                total = total + rbuf[k, h * per_owner + i]
            out_ref[i, :, field] = total

        for i, source, holder, spot in ((0, 1, 0, 0), (1, n - 2, hs - 1, per_owner - 1)):
            @pl.when(my_harm == holder)
            def _(i=i, source=source, spot=spot):
                def wait_edge(h, inner):
                    @pl.when(jnp.logical_or(h != my_harm, me != source))
                    def _():
                        slab_e(k, 0, h, i).wait_recv()

                    return inner

                lax.fori_loop(0, hs, wait_edge, 0)
                total = out_ref[spot, :, field]
                for h in range(hs):
                    total = total + rbuf_e[k, i * hs + h]
                out_ref[spot, :, field] = total

        return carry

    lax.fori_loop(0, FIELDS, collect, 0)

    def drain_slabs(k, carry):
        each_target(k, lambda copy: copy.wait_send())
        return carry

    lax.fori_loop(0, FIELDS, drain_slabs, 0)

    def drain(i, carry):
        block = i // FIELDS
        k = i % FIELDS

        @pl.when(jnp.logical_not(jnp.logical_or(
            jnp.logical_and(first, block == n - 1), jnp.logical_and(last, block == 0))))
        def _():
            to_core(block, k).wait_send()

        @pl.when(jnp.logical_and(
            jnp.logical_and(block <= me, me < n - 1),
            jnp.logical_and(
                jnp.logical_or(me < n - 2, block > 0),
                jnp.logical_not(first))))
        def _():
            to_right(block, k).wait_send()

        @pl.when(jnp.logical_and(
            jnp.logical_and(block >= me, me > 0),
            jnp.logical_and(
                jnp.logical_or(me > 1, block < n - 1),
                jnp.logical_not(last))))
        def _():
            to_left(block, k).wait_send()

        return carry

    lax.fori_loop(0, n * FIELDS, drain, 0)

    def drain_adjoint(k, carry):
        adjoint_to_core(k).wait_send()

        @pl.when(jnp.logical_or(first, last))
        def _():
            edge(k, me).wait_send()

        @pl.when(helper)
        def _():
            edge_to_core(k).wait_send()

        return carry

    lax.fori_loop(0, FIELDS, drain_adjoint, 0)

    @pl.when(jnp.logical_or(first, last))
    def _():
        edge_slots(me).wait_send()


def body(hs, direct_field, adjoint_field, triad_slots):
    n = triad_slots.shape[1]
    kh = direct_field.shape[0]
    nx = direct_field.shape[4]
    wide = kh * SLOTS * 2
    chunk = min(256, wide * nx)
    cells = nx // n
    per_owner = n // hs
    f32, bf16 = jnp.float32, jnp.bfloat16
    dma = pltpu.SemaphoreType.DMA
    slab_shape = (SLOTS * 2, cells, 128)
    block = (FIELDS, wide, nx, 128)
    stage = [
        pltpu.VMEM((2 * wide, nx, 128), f32),
        pltpu.VMEM((FIELDS * wide, nx, 128), f32),
        pltpu.VMEM((FIELDS * wide, nx, 128), f32),
    ]
    c = FIELDS
    out = pl.pallas_call(
        functools.partial(kernel, n, hs, kh, nx),
        out_shape=jax.ShapeDtypeStruct((per_owner, SLOTS * 2, FIELDS, cells, 128), f32),
        in_specs=[pl.BlockSpec(memory_space=pltpu.SMEM)] + [pl.BlockSpec(memory_space=pltpu.HBM)] * 2,
        out_specs=pl.BlockSpec(memory_space=pltpu.VMEM),
        scratch_shapes=[pltpu.VMEM((n,) + block, bf16)] * 2
        + [pltpu.VMEM(block, bf16)] * 4
        + stage * 4
        + [pltpu.VMEM((FIELDS * SLOTS * 2, nx, 128), f32)] * 2
        + [
            pltpu.VMEM((c, n) + slab_shape, f32),
            pltpu.VMEM((c, n) + slab_shape, f32),
            pltpu.VMEM((c, hs * per_owner) + slab_shape, f32),
            pltpu.VMEM((c, 2 * hs) + slab_shape, f32),
            pltpu.VMEM((256, 128), bf16),
            pltpu.VMEM((chunk, chunk), bf16),
            pltpu.SMEM((SLOTS, 2, n), jnp.int32),
            dma((c,)), dma((c,)),
            dma((n, c)), dma((n, c)), dma((n, c)), dma((n, c)),
            dma((n, c)), dma((n, c)), dma((c,)), dma((c,)),
            dma((c,)), dma((c,)), dma((c,)), dma((c,)), dma((2,)),
            dma((c, n)), dma((c, hs * per_owner)), dma((c, n)), dma((c, 2 * hs)),
        ],
        compiler_params=pltpu.CompilerParams(
            collective_id=0, has_side_effects=True, vmem_limit_bytes=56_000_000),
    )(
        jnp.transpose(triad_slots, (0, 2, 1)),
        direct_field.reshape(wide, FIELDS, nx, 128),
        adjoint_field.reshape(wide, FIELDS, nx, 128),
    )
    return out.reshape(per_owner * SLOTS, 2, FIELDS, cells, 128)


def solution(mesh):
    return jax.shard_map(
        functools.partial(body, mesh.shape["harm"]),
        mesh=mesh,
        in_specs=(
            P(("case", "harm"), "mode", None, None, None, "rad"),
            P(("case", "harm"), "mode", None, None, None, "rad"),
            P("mode", None, None),
        ),
        out_specs=P(("case", "harm"), None, None, "mode", "rad"),
        check_vma=False,
    )
```

time: 55.1 us -> 51 us (0.926)
  Pallas kernels: 53.2 us -> 49.4 us
    pallas_call x1, Pallas kernels: 53.2 us -> 49.4 us  [body(): pl.pallas_call(functools.partial(kernel, n, hs, kh, nx), out_shape=jax.Sh...]
where the time goes in v4:
time: 51 us; the launch traced here: 50.8 us
  Pallas kernels  49.4 us (97%)
  local copies, waits for them, and re-layouts  1.36 us (3%)
    pallas_call x1, Pallas kernels, body(): pl.pallas_call(functools.partial(kernel, n, hs, kh, nx), out_shape=jax.Sh...  49.4 us
    unnamed x3, local copies, waits for them, and re-layouts  1.36 us

profile of v4, /device:TPU:0, one launch (start us, length us, event | category | flops | bytes accessed | tf_op | source)
XLA Modules:
  0.0 50.8 jit_solution(5888916425010045051)
XLA Ops:
  0.0 0.0 copy-start
  0.0 0.7 %copy-done = s32[4,4,2]{1,2,0:T(2,128)S(1)} copy-done((s32[4,4,2]{1,2,0:T(2,128)S(1)}, s32[4,4,2]{1,2,0:T(2,128)}, u32[]{:S(2)}) %copy-start) | copy-done | bytes 152
  0.7 49.4 %shard_map.37 = f32[2,8,5,4,128]{4,3,2,1,0:T(4,128)S(1)} custom-call(s32[4,2,4]{2,1,0:T(2,128)S(1)} %bitcast.5, bf16[32,5,16,128]{3,2,1,0:T(8,128)(2,1)} %bitcast.6, bf16[32,5,16,128]{3,2,1,0:T(8,128)(2,1)} %bitcast.7), custom_call_target="tpu_custom_call" | custom-call | tf_op jit(solution)/shard_map/pallas_call | solution.py:476
  50.1 0.7 %copy.5 = f32[8,2,5,4,128]{4,3,2,1,0:T(4,128)} copy(f32[8,2,5,4,128]{4,3,2,1,0:T(4,128)S(1)} %bitcast.4) | data formatting | bytes 327680
Async XLA Ops:
  0.0 0.7 %copy-start = (s32[4,4,2]{1,2,0:T(2,128)S(1)}, s32[4,4,2]{1,2,0:T(2,128)}, u32[]{:S(2)}) copy-start(s32[4,4,2]{1,2,0:T(2,128)} %param.5) | copy-start | bytes 388

commit v5 on v4

--- a/solution.py
+++ b/solution.py
@@ -28,12 +28,13 @@
     slots, d_hbm, a_hbm, out_ref,
     gbuf, pbuf, abuf, apbuf, ebuf, epbuf,
     d_st, dx_st, dr_st, f_st, fx_st, fr_st, a_st, ax_st, ar_st, e_st, ex_st, er_st,
-    run, run_e, sbuf, sbuf_e, rbuf, rbuf_e, radial, axial, slots_e,
+    run, run_e, sbuf, sbuf_e, xbuf, xbuf_e, tbuf, tbuf_e, rbuf, rbuf_e, radial, axial, slots_e,
     local_d, local_a,
     right_send, right_recv, left_send, left_recv,
     core_send, core_recv, adj_send, adj_recv,
     edge_send, edge_recv, edge_core_send, edge_core_recv, slots_sem,
     slab_send, slab_recv, slab_send_e, slab_recv_e,
+    cross_send, cross_recv, cross_send_e, cross_recv_e,
 ):
     me = lax.axis_index("mode")
     my_harm = lax.axis_index("harm")
@@ -285,13 +286,15 @@
     side = jnp.where(low_helper, 0, 1)
     owner_e = jnp.where(low_helper, 0, hs - 1)
 
+    piece = SLOTS * 2 // hs
+
     def slab(k, q, h, i):
-        return remote(sbuf.at[k, q], rbuf.at[k, h * per_owner + i],
+        return remote(tbuf.at[k, q], rbuf.at[k, i, pl.ds(h * piece, piece)],
                       slab_send.at[k, q], slab_recv.at[k, h * per_owner + i],
                       {"mode": q, "harm": owner})
 
     def slab_e(k, q, h, i):
-        return remote(sbuf_e.at[k, q], rbuf_e.at[k, i * hs + h],
+        return remote(tbuf_e.at[k, q], rbuf_e.at[k, i, pl.ds(h * piece, piece)],
                       slab_send_e.at[k, q], slab_recv_e.at[k, i * hs + h],
                       {"mode": q, "harm": owner_e})
 
@@ -309,25 +312,64 @@
 
         lax.fori_loop(0, n, step, 0)
 
-    def deliver(k):
+    def cross(k, target, sender):
+        return remote(sbuf.at[k, :, pl.ds(target * piece, piece)], xbuf.at[k, sender],
+                      cross_send.at[k, target], cross_recv.at[k, sender], {"harm": target})
+
+    def cross_e(k, target, sender):
+        return remote(sbuf_e.at[k, :, pl.ds(target * piece, piece)], xbuf_e.at[k, sender],
+                      cross_send_e.at[k, target], cross_recv_e.at[k, sender], {"harm": target})
+
+    def each_partner(act):
+        def step(h, carry):
+            @pl.when(h != my_harm)
+            def _():
+                act(h)
+
+            return carry
+
+        lax.fori_loop(0, hs, step, 0)
+
+    own_piece = pl.ds(my_harm * piece, piece)
+
+    def share(k):
         span = pl.ds(k * SLOTS * 2, SLOTS * 2)
         for q in range(n):
             sbuf[k, q] = run[span, q * cells:(q + 1) * cells, :] * scale
+        each_partner(lambda h: cross(k, h, my_harm).start())
+        xbuf[k, my_harm] = sbuf[k, :, own_piece]
 
         @pl.when(helper)
         def _():
             for q in range(n):
                 sbuf_e[k, q] = run_e[span, q * cells:(q + 1) * cells, :] * scale
+            each_partner(lambda h: cross_e(k, h, my_harm).start())
+            xbuf_e[k, my_harm] = sbuf_e[k, :, own_piece]
+
+    def deliver(k):
+        each_partner(lambda h: cross(k, h, h).wait_recv())
+        total = xbuf[k, 0]
+        for h in range(1, hs):
+            total = total + xbuf[k, h]
+        tbuf[k] = total
+
+        @pl.when(helper)
+        def _():
+            each_partner(lambda h: cross_e(k, h, h).wait_recv())
+            total = xbuf_e[k, 0]
+            for h in range(1, hs):
+                total = total + xbuf_e[k, h]
+            tbuf_e[k] = total
 
         each_target(k, lambda copy: copy.start())
 
         @pl.when(owner == my_harm)
         def _():
-            rbuf[k, my_harm * per_owner + place] = sbuf[k, me]
+            rbuf[k, place, own_piece] = tbuf[k, me]
 
         @pl.when(jnp.logical_and(helper, owner_e == my_harm))
         def _():
-            rbuf_e[k, side * hs + my_harm] = sbuf_e[k, me]
+            rbuf_e[k, side, own_piece] = tbuf_e[k, me]
 
     def own_chunk(k, carry):
         adjoint_to_core(k).wait_recv()
@@ -354,11 +396,16 @@
 
         @pl.when(i > count - FIELDS)
         def _():
-            ready(i - 1 - (count - FIELDS), deliver)
+            ready(i - 1 - (count - FIELDS), share)
+
+        @pl.when(i > count - FIELDS + 1)
+        def _():
+            ready(i - 2 - (count - FIELDS), deliver)
 
         return carry
 
     lax.fori_loop(0, count + 1, steps, 0)
+    deliver(FIELDS - 1)
 
     def collect(k, carry):
         def arrive(index, inner):
@@ -375,10 +422,7 @@
         lax.fori_loop(0, hs * per_owner, arrive, 0)
         field = jnp.where(k < 2, k + 1, jnp.where(k == 2, 0, k))
         for i in range(per_owner):
-            total = rbuf[k, i]
-            for h in range(1, hs):
-                total = total + rbuf[k, h * per_owner + i]
-            out_ref[i, :, field] = total
+            out_ref[i, :, field] = rbuf[k, i]
 
         for i, source, holder, spot in ((0, 1, 0, 0), (1, n - 2, hs - 1, per_owner - 1)):
             @pl.when(my_harm == holder)
@@ -391,10 +435,7 @@
                     return inner
 
                 lax.fori_loop(0, hs, wait_edge, 0)
-                total = out_ref[spot, :, field]
-                for h in range(hs):
-                    total = total + rbuf_e[k, i * hs + h]
-                out_ref[spot, :, field] = total
+                out_ref[spot, :, field] = out_ref[spot, :, field] + rbuf_e[k, i]
 
         return carry
 
@@ -402,6 +443,12 @@
 
     def drain_slabs(k, carry):
         each_target(k, lambda copy: copy.wait_send())
+        each_partner(lambda h: cross(k, h, my_harm).wait_send())
+
+        @pl.when(helper)
+        def _():
+            each_partner(lambda h: cross_e(k, h, my_harm).wait_send())
+
         return carry
 
     lax.fori_loop(0, FIELDS, drain_slabs, 0)
@@ -466,6 +513,7 @@
     f32, bf16 = jnp.float32, jnp.bfloat16
     dma = pltpu.SemaphoreType.DMA
     slab_shape = (SLOTS * 2, cells, 128)
+    piece = SLOTS * 2 // hs
     block = (FIELDS, wide, nx, 128)
     stage = [
         pltpu.VMEM((2 * wide, nx, 128), f32),
@@ -485,8 +533,12 @@
         + [
             pltpu.VMEM((c, n) + slab_shape, f32),
             pltpu.VMEM((c, n) + slab_shape, f32),
-            pltpu.VMEM((c, hs * per_owner) + slab_shape, f32),
-            pltpu.VMEM((c, 2 * hs) + slab_shape, f32),
+            pltpu.VMEM((c, hs, n, piece) + slab_shape[1:], f32),
+            pltpu.VMEM((c, hs, n, piece) + slab_shape[1:], f32),
+            pltpu.VMEM((c, n, piece) + slab_shape[1:], f32),
+            pltpu.VMEM((c, n, piece) + slab_shape[1:], f32),
+            pltpu.VMEM((c, per_owner) + slab_shape, f32),
+            pltpu.VMEM((c, 2) + slab_shape, f32),
             pltpu.VMEM((256, 128), bf16),
             pltpu.VMEM((chunk, chunk), bf16),
             pltpu.SMEM((SLOTS, 2, n), jnp.int32),
@@ -495,6 +547,7 @@
             dma((n, c)), dma((n, c)), dma((c,)), dma((c,)),
             dma((c,)), dma((c,)), dma((c,)), dma((c,)), dma((2,)),
             dma((c, n)), dma((c, hs * per_owner)), dma((c, n)), dma((c, 2 * hs)),
+            dma((c, hs)), dma((c, hs)), dma((c, hs)), dma((c, hs)),
         ],
         compiler_params=pltpu.CompilerParams(
             collective_id=0, has_side_effects=True, vmem_limit_bytes=56_000_000),

time: 51 us -> 55.5 us (1.088)
  Pallas kernels: 49.4 us -> 54 us
    pallas_call x1, Pallas kernels: 49.4 us -> 54 us  [body(): pl.pallas_call(functools.partial(kernel, n, hs, kh, nx), out_shape=jax.Sh...]
where the time goes in v5:
time: 55.5 us; the launch traced here: 55.3 us
  Pallas kernels  54 us (97%)
  local copies, waits for them, and re-layouts  1.36 us (2%)
    pallas_call x1, Pallas kernels, body(): pl.pallas_call(functools.partial(kernel, n, hs, kh, nx), out_shape=jax.Sh...  54 us
    unnamed x3, local copies, waits for them, and re-layouts  1.36 us

profile of v5, /device:TPU:0, one launch (start us, length us, event | category | flops | bytes accessed | tf_op | source)
XLA Modules:
  0.0 55.3 jit_solution(169131896924645899)
XLA Ops:
  0.0 0.0 copy-start
  0.0 0.7 %copy-done = s32[4,4,2]{1,2,0:T(2,128)S(1)} copy-done((s32[4,4,2]{1,2,0:T(2,128)S(1)}, s32[4,4,2]{1,2,0:T(2,128)}, u32[]{:S(2)}) %copy-start) | copy-done | bytes 152
  0.7 54.0 %shard_map.37 = f32[2,8,5,4,128]{4,3,2,1,0:T(4,128)S(1)} custom-call(s32[4,2,4]{2,1,0:T(2,128)S(1)} %bitcast.5, bf16[32,5,16,128]{3,2,1,0:T(8,128)(2,1)} %bitcast.6, bf16[32,5,16,128]{3,2,1,0:T(8,128)(2,1)} %bitcast.7), custom_call_target="tpu_custom_call" | custom-call | tf_op jit(solution)/shard_map/pallas_call | solution.py:524
  54.7 0.7 %copy.5 = f32[8,2,5,4,128]{4,3,2,1,0:T(4,128)} copy(f32[8,2,5,4,128]{4,3,2,1,0:T(4,128)S(1)} %bitcast.4) | data formatting | bytes 327680
Async XLA Ops:
  0.0 0.7 %copy-start = (s32[4,4,2]{1,2,0:T(2,128)S(1)}, s32[4,4,2]{1,2,0:T(2,128)}, u32[]{:S(2)}) copy-start(s32[4,4,2]{1,2,0:T(2,128)} %param.5) | copy-start | bytes 388

commit v6 on v4

--- a/solution.py
+++ b/solution.py
@@ -155,7 +155,7 @@
                 axial[...], mine, preferred_element_type=jnp.float32).reshape(shape)
             return carry
 
-        lax.fori_loop(0, wide // group, step, 0)
+        lax.fori_loop(0, wide // group, step, 0, unroll=True)
 
     def products(table, stop, total, dirs, adjs, k):
         d_pl, d_x, d_r = dirs
@@ -296,7 +296,9 @@
                       {"mode": q, "harm": owner_e})
 
     def each_target(k, act):
-        def step(q, carry):
+        def step(index, carry):
+            q = jnp.where(me < n // 2, n - 1 - index, index)
+
             @pl.when(jnp.logical_or(q != me, owner != my_harm))
             def _():
                 act(slab(k, q, my_harm, place))

time: 51 us -> 51.1 us (level)
  no operation moved by 1% of the time
where the time goes in v6:
time: 51.1 us; the launch traced here: 50.9 us
  Pallas kernels  49.5 us (97%)
  local copies, waits for them, and re-layouts  1.36 us (3%)
    pallas_call x1, Pallas kernels, body(): pl.pallas_call(functools.partial(kernel, n, hs, kh, nx), out_shape=jax.Sh...  49.5 us
    unnamed x3, local copies, waits for them, and re-layouts  1.36 us

profile of v6, /device:TPU:0, one launch (start us, length us, event | category | flops | bytes accessed | tf_op | source)
XLA Modules:
  0.0 50.9 jit_solution(13625129933954674066)
XLA Ops:
  0.0 0.0 copy-start
  0.0 0.7 %copy-done = s32[4,4,2]{1,2,0:T(2,128)S(1)} copy-done((s32[4,4,2]{1,2,0:T(2,128)S(1)}, s32[4,4,2]{1,2,0:T(2,128)}, u32[]{:S(2)}) %copy-start) | copy-done | bytes 152
  0.7 49.5 %shard_map.37 = f32[2,8,5,4,128]{4,3,2,1,0:T(4,128)S(1)} custom-call(s32[4,2,4]{2,1,0:T(2,128)S(1)} %bitcast.5, bf16[32,5,16,128]{3,2,1,0:T(8,128)(2,1)} %bitcast.6, bf16[32,5,16,128]{3,2,1,0:T(8,128)(2,1)} %bitcast.7), custom_call_target="tpu_custom_call" | custom-call | tf_op jit(solution)/shard_map/pallas_call | solution.py:478
  50.2 0.7 %copy.5 = f32[8,2,5,4,128]{4,3,2,1,0:T(4,128)} copy(f32[8,2,5,4,128]{4,3,2,1,0:T(4,128)S(1)} %bitcast.4) | data formatting | bytes 327680
Async XLA Ops:
  0.0 0.7 %copy-start = (s32[4,4,2]{1,2,0:T(2,128)S(1)}, s32[4,4,2]{1,2,0:T(2,128)}, u32[]{:S(2)}) copy-start(s32[4,4,2]{1,2,0:T(2,128)} %param.5) | copy-start | bytes 388
